TPU v7x, 768 devices: a whole 4x8x12 slice. The times are simulated.
768 devices in a mesh: dp: 128 (over x, y, z_hi), tensor: 6 (over z_lo, core).
Axes of the slice: x: 4, y: 8, z: 12 (z_hi: 4, z_lo: 3; z = z_hi * 3 + z_lo), core: 2. Of those that a mesh axis runs over, the one named last changes fastest.
Arguments:
- hidden: bfloat16 [18432, 4096], P(('dp', 'tensor')), may hold values from -6 to 6
- doc_ids: int32 [128, 144], replicated, may hold values from 0 to 3, never falling along the last dimension, each value on 1 to 72 neighbouring positions
- teacher: bfloat16 [18432, 8448], P('dp', 'tensor'), may hold values from -6 to 6
- rotation: int32 [1], replicated, may hold values from 0 to 127
- norm_gain_vector: float32 [4096], replicated, may hold values from 0.5 to 1.5
- proj_bias: float32 [8448], P('tensor'), may hold values from -3 to 3
- projection: bfloat16 [4096, 8448], P(None, 'tensor'), may hold values from -0.09375 to 0.09375
Outputs:
- hidden_gradient: bfloat16 [18432, 4096], P(('dp', 'tensor'))
- gain_gradient_mean: float32 [4096], replicated
- grad_bias: float32 [8448], P('tensor')
- distill_loss: float32 [], replicated
Inputs may be any that keep to these rules, and one draw needn't show every extreme that they name: `doc_ids`: in each row the document numbers never fall; each document has 1 to 72 tokens and one has exactly 72.
All inputs are finite; a program needn't handle non-finite values.
Results may differ from a plain program's by a relative error of at most 0.0049.
The roundings to bfloat16 on the way count: a program that leaves them out, or rounds other values in their place, can miss the bound.
Values may be sent and summed in bfloat16 or wider, within the bound.
No kernel may reach another device: no remote copies, remote signals or barrier semaphores. Data moves between devices by JAX's collectives and lax.ppermute only.
A program may use at most 64 MiB of HBM per device.

v0:
```python
import jax
import jax.numpy as jnp
import numpy as np
from jax import lax
from jax.sharding import Mesh, PartitionSpec as P


DOCS = 4
NORM_EPS = 1e-05

AXES = ("x", "y", "zh", "zl", "c")
SIZES = (4, 8, 4, 3, 2)
DP = ("x", "y", "zh")
TENSOR = ("zl", "c")
N_X, N_Y, N_ZH, N_ZL, N_C = SIZES
N_DP = N_X * N_Y * N_ZH
LANES = 128


def pull(value, steps):
    return lax.ppermute(value, DP, [((i + steps) % N_DP, i) for i in range(N_DP)])


def swap_cores(value):
    return lax.ppermute(value, "c", [(0, 1), (1, 0)])


def spread(value, axes, count):
    copies = lax.optimization_barrier(jnp.broadcast_to(value[None], (count, *value.shape)))
    return lax.all_to_all(copies, axes, 0, 0, tiled=True)


def own_first(value, core):
    parts = value.reshape(N_ZL, N_C, -1, *value.shape[1:])
    half = (value.shape[0] // N_C, *value.shape[1:])
    even, odd = parts[:, 0].reshape(half), parts[:, 1].reshape(half)
    first = core == 0
    return jnp.concatenate([jnp.where(first, even, odd), jnp.where(first, odd, even)], 0)


def normalized(rows):
    entries = rows.astype(jnp.float32)
    inverse = lax.rsqrt(jnp.mean(entries * entries, axis=-1, keepdims=True) + NORM_EPS)
    return entries * inverse, inverse


def shards(hidden, doc_ids, teacher, rotation, gain, bias, projection):
    core = lax.axis_index("c")
    here = (lax.axis_index("x") * N_Y + lax.axis_index("y")) * N_ZH + lax.axis_index("zh")
    turn = rotation[0] % N_DP
    portion_rows, width = hidden.shape
    block_rows = teacher.shape[0]
    columns = projection.shape[1]
    tokens = block_rows * N_DP
    features = columns * N_ZL * N_C

    gathered = spread(hidden, "zl", N_ZL)

    far = [lambda t, s=s: pull(t, s * N_ZH) if s else t for s in range(N_X * N_Y)]
    moved = lax.switch(turn // N_ZH, far, teacher)

    row_docs = lax.dynamic_slice_in_dim(doc_ids, here, 1, 0)[0]
    same_doc = jnp.sum((row_docs[:, None] == row_docs[None, :]).astype(jnp.float32), axis=-1)
    weight = own_first((block_rows / (DOCS * same_doc))[:, None], core)

    def near(step):
        def branch(t, mine, weight):
            target = pull(t, step) if step else t
            mine = mine.reshape(-1, width)
            other = swap_cores(mine)
            block = jnp.concatenate([mine, other], 0)
            unscaled, inverse = normalized(block)
            rows = (unscaled * gain).astype(jnp.bfloat16)
            logits = jnp.dot(rows, projection, preferred_element_type=jnp.float32) + bias
            logits = lax.optimization_barrier(logits)
            error = logits - own_first(target, core).astype(jnp.float32)
            loss_part = jnp.sum(weight * error * error) / (2.0 * tokens * features)
            grad_out = (weight * error).astype(jnp.bfloat16)
            bias_part = jnp.sum(grad_out.astype(jnp.float32), axis=0) / tokens
            return lax.optimization_barrier((grad_out, loss_part, bias_part, other, inverse))

        return branch

    grad_out, loss_part, bias_part, other, block_inverse = lax.switch(
        turn % N_ZH, [near(s) for s in range(N_ZH)], moved, gathered, weight
    )
    grad_all = lax.dot_general(
        grad_out, projection, (((1,), (1,)), ((), ())), preferred_element_type=jnp.float32
    )
    block = jnp.concatenate([gathered.reshape(-1, width), other], 0)
    gain_part = jnp.sum(grad_all * (block.astype(jnp.float32) * block_inverse), axis=0) / tokens

    half = block_rows // N_C
    summed = grad_all[:half] + swap_cores(grad_all[half:].astype(jnp.bfloat16)).astype(jnp.float32)
    summed = summed.reshape(N_ZL, portion_rows, width)
    at = lax.axis_index("zl")
    portion_gradient = lax.dynamic_index_in_dim(summed, at, 0, keepdims=False)
    for step in range(1, N_ZL):
        piece = lax.dynamic_index_in_dim(summed, (at + step) % N_ZL, 0, keepdims=False)
        ring = [(i, (i + step) % N_ZL) for i in range(N_ZL)]
        piece = lax.ppermute(piece.astype(jnp.bfloat16), "zl", ring)
        portion_gradient = portion_gradient + piece.astype(jnp.float32)

    n_tensor = N_ZL * N_C
    peers = N_X * n_tensor
    gain_lines, bias_lines = width // LANES, columns // LANES
    gain_each, bias_each = -(-(gain_lines + 1) // peers), -(-bias_lines // N_X)
    used = gain_each + bias_each
    each = -(-used // 8) * 8
    shared = jnp.concatenate(
        [
            gain_part.reshape(gain_lines, LANES),
            jnp.broadcast_to(loss_part, (1, LANES)),
            jnp.zeros((peers * gain_each - gain_lines - 1, LANES), jnp.float32),
        ],
        0,
    ).reshape(peers, gain_each, LANES)
    by_x = jnp.pad(bias_part.reshape(bias_lines, LANES), ((0, N_X * bias_each - bias_lines), (0, 0)))
    by_x = jnp.broadcast_to(by_x.reshape(N_X, 1, bias_each, LANES), (N_X, n_tensor, bias_each, LANES))
    lines = jnp.concatenate(
        [
            shared,
            by_x.reshape(peers, bias_each, LANES),
            jnp.zeros((peers, each - used, LANES), jnp.float32),
        ],
        1,
    )
    group = ("x", *TENSOR)
    column = lax.axis_index("zl") * N_C + core
    lines = lax.all_to_all(lines, group, 0, 0, tiled=True)
    line = lax.broadcasted_iota(jnp.int32, lines.shape, 1)
    sender = lax.broadcasted_iota(jnp.int32, lines.shape, 0) % n_tensor
    lines = jnp.sum(jnp.where((line < gain_each) | (sender == column), lines, 0.0), axis=0)
    lines = jnp.sum(spread(lines, ("y", "zh"), N_Y * N_ZH), axis=0)
    lines = spread(lines, group, peers)
    shared = lines[:, :gain_each].reshape(peers * gain_each, LANES)
    gain_gradient_mean = shared[:gain_lines].reshape(width)
    distill_loss = shared[gain_lines, 0]
    by_x = lax.dynamic_slice_in_dim(
        lines[:, gain_each:used].reshape(N_X, n_tensor, bias_each, LANES), column, 1, 1
    )
    grad_bias = by_x.reshape(N_X * bias_each, LANES)[:bias_lines].reshape(columns)

    unscaled, inverse = normalized(hidden)
    unscaled_gradient = portion_gradient * gain
    inner = jnp.mean(unscaled_gradient * unscaled, axis=-1, keepdims=True)
    hidden_gradient = (inverse * (unscaled_gradient - unscaled * inner)).astype(jnp.bfloat16)
    return (hidden_gradient, gain_gradient_mean, grad_bias, distill_loss)


def solution(mesh):
    split = Mesh(np.asarray(mesh.devices).reshape(SIZES), AXES)
    return jax.shard_map(
        shards,
        mesh=split,
        in_specs=(P(AXES, None), P(), P(DP, TENSOR), P(), P(), P(TENSOR), P(None, TENSOR)),
        out_specs=(P(AXES, None), P(), P(TENSOR), P()),
        check_vma=False,
    )
```

profile of v0, /device:TPU:1, one launch (start us, length us, event | category | flops | bytes accessed | tf_op | source)
XLA Modules:
  0.0 174.9 jit_solution(14101968896795296291)
XLA Ops:
  0.6 0.0 copy-start
  0.6 0.0 copy-start.3
  0.7 1.8 %broadcast_in_dim.31 = bf16[3,24,4096]{2,1,0:T(8,128)(2,1)} broadcast(bf16[24,4096]{1,0:T(8,128)(2,1)} %param.43), dimensions={1,2} | broadcast | bytes 786432 | tf_op jit(solution)/shard_map/broadcast_in_dim | solution.py:29
  2.5 6.0 %all-to-all-start = ((bf16[3,24,4096]{2,1,0:T(8,128)(2,1)}), bf16[3,24,4096]{2,1,0:T(8,128)(2,1)S(1)}, u32[]{:S(2)}, u32[]{:S(2)}) async-start(bf16[3,24,4096]{2,1,0:T(8,128)(2,1)} %broadcast_in_dim.31), calls=%async_computation | async-start | bytes 1179648 | tf_op jit(solution)/shard_map/all_to_all | solution.py:30
  9.2 0.0 copy-done
  9.2 0.2 dynamic-slice_reduce_fusion
  9.4 0.2 convert_reduce_fusion.4
  9.6 0.1 div.77
  9.7 0.1 select_n.154
  9.8 0.1 select_n.156
  9.9 0.1 pad.26.clone
  10.0 0.1 pad.23.clone
  10.0 0.0 copy-done.3
  10.1 0.0 copy-start.4
  10.1 0.0 copy-start.5
  10.1 27.4 %conditional.2 = (bf16[144,1408]{1,0:T(8,128)(2,1)S(1)}) conditional(s32[]{:T(128)} %clamp.7, bf16[144,1408]{1,0:T(8,128)(2,1)S(1)} %copy-done.3, bf16[144,1408]{1,0:T(8,128)(2,1)S(1)} %copy-done.3, bf16[144,1408]{1,0:T(8,128)(2,1)S(1)} %copy-done.3, bf16[144,1408]{1,0:T(8,128)(2,1)S(1)} %copy-done.3, ...), branch_computations={%region_1.2_spmd, %region_2.3_spmd, %region_3.4_spmd, %region_4.5_... | conditional | bytes 2433072 | solution.py:60
  10.1 6.7 %collective-permute-start.26 = (bf16[144,1408]{1,0:T(8,128)(2,1)S(1)}, bf16[144,1408]{1,0:T(8,128)(2,1)S(1)}, u32[]{:S(2)}, u32[]{:S(2)}) collective-permute-start(bf16[144,1408]{1,0:T(8,128)(2,1)S(1)} %param.27), channel_id=1, source_target_pairs={{648,0},{654,6},{660,12},{666,18},{672,24},{678,30},{684,36},{690,... | collective-permute-start | bytes 1216520 | tf_op jit(solution)/shard_map/cond/branch_27_fun/ppermute | solution.py:21
  16.8 20.7 %collective-permute-done.26 = bf16[144,1408]{1,0:T(8,128)(2,1)S(1)} collective-permute-done((bf16[144,1408]{1,0:T(8,128)(2,1)S(1)}, bf16[144,1408]{1,0:T(8,128)(2,1)S(1)}, u32[]{:S(2)}, u32[]{:S(2)}) %collective-permute-start.26) | collective-permute-done | bytes 405536 | tf_op jit(solution)/shard_map/cond/branch_27_fun/ppermute | solution.py:21
  37.5 0.1 pad_maximum_fusion.12
  37.6 0.0 all-to-all-done
  37.6 0.0 copy-done.4
  37.6 0.0 copy-done.5
  37.6 75.3 %conditional.3 = (bf16[144,1408]{1,0:T(8,128)(2,1)S(1)}, f32[]{:T(128)}, f32[1408]{0:T(1024)S(1)}, bf16[72,4096]{1,0:T(8,128)(2,1)}, f32[144,1]{0,1:T(1,128)}) conditional(s32[]{:T(128)} %clamp.6, (f32[144,1]{0,1:T(1,128)S(1)}, bf16[3,24,4096]{2,1,0:T(8,128)(2,1)S(1)}, f32[4096]{0:T(1024)S(1)}, ...), branch_computations={%region_34.0_spmd, %region_38.42_spmd, %region_42.46_spmd, %region... | conditional | flops 1671248000 | bytes 21160912 | solution.py:84
  37.6 27.3 %collective-permute-start.35 = (bf16[144,1408]{1,0:T(8,128)(2,1)S(1)}, bf16[144,1408]{1,0:T(8,128)(2,1)S(1)}, u32[]{:S(2)}, u32[]{:S(2)}) collective-permute-start(bf16[144,1408]{1,0:T(8,128)(2,1)S(1)} %get-tuple-element.141), channel_id=1, source_target_pairs={{12,0},{18,6},{24,12},{30,18},{36,24},{42,30},{48,36},{54,42},{60,... | collective-permute-start | bytes 1216520 | tf_op jit(solution)/shard_map/cond/branch_2_fun/ppermute | solution.py:21
  64.9 8.5 %collective-permute-start.34 = (bf16[72,4096]{1,0:T(8,128)(2,1)S(1)}, bf16[72,4096]{1,0:T(8,128)(2,1)}, u32[]{:S(2)}, u32[]{:S(2)}) collective-permute-start(bf16[72,4096]{1,0:T(8,128)(2,1)S(1)} %bitcast.118), channel_id=1, source_target_pairs={{0,1},{1,0},{2,3},{3,2},{4,5},{5,4},{6,7},{7,6},{8,9},{9,8},{10,11... | collective-permute-start | bytes 1769480 | tf_op jit(solution)/shard_map/cond/branch_2_fun/ppermute | solution.py:25
  73.4 28.8 %collective-permute-done.35 = bf16[144,1408]{1,0:T(8,128)(2,1)S(1)} collective-permute-done((bf16[144,1408]{1,0:T(8,128)(2,1)S(1)}, bf16[144,1408]{1,0:T(8,128)(2,1)S(1)}, u32[]{:S(2)}, u32[]{:S(2)}) %collective-permute-start.35) | collective-permute-done | bytes 405536 | tf_op jit(solution)/shard_map/cond/branch_2_fun/ppermute | solution.py:21
  102.2 0.0 collective-permute-done.34
  102.2 1.4 fusion.16
  103.6 0.6 add_rsqrt_fusion.2
  104.2 6.6 %convolution_add_fusion.2 = f32[144,1408]{1,0:T(8,128)S(1)} fusion(bf16[4096,1408]{1,0:T(8,128)(2,1)} %get-tuple-element.138, f32[4096]{0:T(1024)S(1)} %get-tuple-element.137, f32[144]{0:T(256)} %add_rsqrt_fusion.2, bf16[72,4096]{1,0:T(8,128)(2,1)} %collective-permute-done.34, bf16[72,4096]{1,0:T(8,128)(2,1)S(1)} %bitcast.120, f32[1408]{0:T(1024)S(1)} %get-tuple-element.139), kind=kOutput, calls=%fused_computation.46 | convolution fusion | flops 1665275904 | bytes 13547584 | tf_op jit(solution)/shard_map/cond/branch_2_fun/dot_general | solution.py:74
  110.8 1.0 convert_reduce_fusion.2
  112.9 8.2 %multiply_reduce_fusion = (f32[4096]{0:T(1024)S(1)}, f32[144,4096]{1,0:T(8,128)S(1)}) fusion(bf16[72,4096]{1,0:T(8,128)(2,1)} %get-tuple-element.159, bf16[72,4096]{1,0:T(8,128)(2,1)S(1)} %bitcast.111, f32[144]{0:T(256)} %bitcast.30, bf16[144,1408]{1,0:T(8,128)(2,1)S(1)} %get-tuple-element.158, bf16[4096,1408]{1,0:T(8,128)(2,1)} %param.49), kind=kOutput, calls=%fused_computation.88 | convolution fusion | flops 1665069056 | bytes 15495744 | tf_op jit(solution)/shard_map/dot_general | solution.py:87
  121.1 0.1 pad.25.clone
  121.2 0.1 slice.127
  121.3 2.9 %collective-permute-start.38 = (bf16[72,4096]{1,0:T(8,128)(2,1)S(1)}, bf16[72,4096]{1,0:T(8,128)(2,1)}, u32[]{:S(2)}, u32[]{:S(2)}) collective-permute-start(bf16[72,4096]{1,0:T(8,128)(2,1)S(1)} %slice.127), channel_id=1, source_target_pairs={{0,1},{1,0},{2,3},{3,2},{4,5},{5,4},{6,7},{7,6},{8,9},{9,8},{10,11... | collective-permute-start | bytes 1769480 | tf_op jit(solution)/shard_map/ppermute | solution.py:25
  124.2 0.1 maximum_maximum_fusion.1
  124.3 0.7 maximum_maximum_fusion
  125.0 5.5 %all-to-all-start.1 = ((f32[24,8,128]{2,1,0:T(8,128)}), f32[24,8,128]{2,1,0:T(8,128)S(1)}, u32[]{:S(2)}, u32[]{:S(2)}) async-start(f32[24,8,128]{2,1,0:T(8,128)} %maximum_maximum_fusion), calls=%async_computation.1 | async-start | bytes 196608 | tf_op jit(solution)/shard_map/all_to_all | solution.py:130
  130.6 1.1 fusion.38
  131.7 0.0 copy-start.2
  131.7 6.0 %all-to-all-done.1 = f32[24,8,128]{2,1,0:T(8,128)S(1)} async-done(((f32[24,8,128]{2,1,0:T(8,128)}), f32[24,8,128]{2,1,0:T(8,128)S(1)}, u32[]{:S(2)}, u32[]{:S(2)}) %all-to-all-start.1) | async-done | bytes 98336 | tf_op jit(solution)/shard_map/all_to_all | solution.py:130
  137.6 0.1 select_reduce_fusion
  137.8 0.7 broadcast_in_dim.39
  138.5 7.8 %all-to-all-start.2 = ((f32[32,8,128]{2,1,0:T(8,128)}), f32[32,8,128]{2,1,0:T(8,128)S(1)}, u32[]{:S(2)}, u32[]{:S(2)}) async-start(f32[32,8,128]{2,1,0:T(8,128)} %broadcast_in_dim.39), calls=%async_computation.2 | async-start | bytes 262144 | tf_op jit(solution)/shard_map/all_to_all | solution.py:30
  146.2 0.0 collective-permute-done.38
  146.2 1.2 slice_add_fusion
  147.4 0.0 copy-start.1
  147.5 1.0 copy-done.1
  148.5 1.9 %collective-permute-start.39 = (bf16[24,4096]{1,0:T(8,128)(2,1)S(1)}, bf16[24,4096]{1,0:T(8,128)(2,1)S(1)}, u32[]{:S(2)}, u32[]{:S(2)}) collective-permute-start(bf16[24,4096]{1,0:T(8,128)(2,1)S(1)} %get-tuple-element.185), channel_id=1, source_target_pairs={{0,2},{2,4},{4,0},{1,3},{3,5},{5,1},{6,8},{8,10},{10,6},{7,9},{9,1... | collective-permute-start | bytes 589832 | tf_op jit(solution)/shard_map/ppermute | solution.py:101
  150.4 4.3 %collective-permute-start.40 = (bf16[24,4096]{1,0:T(8,128)(2,1)S(1)}, bf16[24,4096]{1,0:T(8,128)(2,1)S(1)}, u32[]{:S(2)}, u32[]{:S(2)}) collective-permute-start(bf16[24,4096]{1,0:T(8,128)(2,1)S(1)} %get-tuple-element.186), channel_id=1, source_target_pairs={{0,4},{2,0},{4,2},{1,5},{3,1},{5,3},{6,10},{8,6},{10,8},{7,11},{9,... | collective-permute-start | bytes 589832 | tf_op jit(solution)/shard_map/ppermute | solution.py:101
  154.7 5.2 %all-to-all-done.2 = f32[32,8,128]{2,1,0:T(8,128)S(1)} async-done(((f32[32,8,128]{2,1,0:T(8,128)}), f32[32,8,128]{2,1,0:T(8,128)S(1)}, u32[]{:S(2)}, u32[]{:S(2)}) %all-to-all-start.2) | async-done | bytes 131104 | tf_op jit(solution)/shard_map/all_to_all | solution.py:30
  160.0 0.7 broadcast_in_dim.40
  160.6 5.3 %all-to-all-start.3 = ((f32[24,8,128]{2,1,0:T(8,128)}), f32[24,8,128]{2,1,0:T(8,128)S(1)}, u32[]{:S(2)}, u32[]{:S(2)}) async-start(f32[24,8,128]{2,1,0:T(8,128)} %broadcast_in_dim.40), calls=%async_computation.3 | async-start | bytes 196608 | tf_op jit(solution)/shard_map/all_to_all | solution.py:30
  165.9 0.0 collective-permute-done.39
  165.9 0.0 collective-permute-done.40
  165.9 0.0 copy-done.2
  165.9 1.3 fusion.34
  167.2 1.8 %fusion.37 = bf16[24,4096]{1,0:T(8,128)(2,1)} fusion(bf16[24,4096]{1,0:T(8,128)(2,1)S(1)} %copy-done.2, f32[24]{0:T(128)S(1)} %broadcast_multiply_fusion.4, f32[24]{0:T(128)S(1)} %add_rsqrt_fusion.4, f32[4096]{0:T(1024)S(1)} %copy-done.4, bf16[24,4096]{1,0:T(8,128)(2,1)S(1)} %collective-permute-done.40, bf16[24,4096]{1,0:T(8,128)(2,1)S(1)} %collective-permute-done.39, ...), kind=kLoop, calls=%fused_computation.98 | loop fusion | flops 1081344 | bytes 1196228 | tf_op jit(solution)/shard_map/convert_element_type | solution.py:147
  169.1 4.1 %all-to-all-done.3 = f32[24,8,128]{2,1,0:T(8,128)S(1)} async-done(((f32[24,8,128]{2,1,0:T(8,128)}), f32[24,8,128]{2,1,0:T(8,128)S(1)}, u32[]{:S(2)}, u32[]{:S(2)}) %all-to-all-start.3) | async-done | bytes 98336 | tf_op jit(solution)/shard_map/all_to_all | solution.py:30
  173.2 0.6 slice_bitcast_fusion.8
  173.8 0.5 slice.79
  174.3 0.6 slice.75
  (22 shorter events, 0.3 us)
Async XLA Ops:
  0.6 8.6 %copy-start = (s32[128,144]{0,1:T(8,128)S(1)}, s32[128,144]{0,1:T(8,128)}, u32[]{:S(2)}) copy-start(s32[128,144]{0,1:T(8,128)} %param.44) | copy-start | bytes 221188
  0.6 9.4 %copy-start.3 = (bf16[144,1408]{1,0:T(8,128)(2,1)S(1)}, bf16[144,1408]{1,0:T(8,128)(2,1)}, u32[]{:S(2)}) copy-start(bf16[144,1408]{1,0:T(8,128)(2,1)} %param.45) | copy-start | bytes 1216516
  2.5 35.1 %all-to-all-start = ((bf16[3,24,4096]{2,1,0:T(8,128)(2,1)}), bf16[3,24,4096]{2,1,0:T(8,128)(2,1)S(1)}, u32[]{:S(2)}, u32[]{:S(2)}) async-start(bf16[3,24,4096]{2,1,0:T(8,128)(2,1)} %broadcast_in_dim.31), calls=%async_computation | async-start | bytes 1179648 | tf_op jit(solution)/shard_map/all_to_all | solution.py:30
  10.1 27.5 %copy-start.4 = (f32[4096]{0:T(1024)S(1)}, f32[4096]{0:T(1024)}, u32[]{:S(2)}) copy-start(f32[4096]{0:T(1024)} %param.47) | copy-start | bytes 49156
  10.1 27.5 %copy-start.5 = (f32[1408]{0:T(1024)S(1)}, f32[1408]{0:T(1024)}, u32[]{:S(2)}) copy-start(f32[1408]{0:T(1024)} %param.48) | copy-start | bytes 16900
  10.1 27.4 %collective-permute-start.26 = (bf16[144,1408]{1,0:T(8,128)(2,1)S(1)}, bf16[144,1408]{1,0:T(8,128)(2,1)S(1)}, u32[]{:S(2)}, u32[]{:S(2)}) collective-permute-start(bf16[144,1408]{1,0:T(8,128)(2,1)S(1)} %param.27), channel_id=1, source_target_pairs={{648,0},{654,6},{660,12},{666,18},{672,24},{678,30},{684,36},{690,... | collective-permute-start | bytes 1216520 | tf_op jit(solution)/shard_map/cond/branch_27_fun/ppermute | solution.py:21
  37.6 64.6 %collective-permute-start.35 = (bf16[144,1408]{1,0:T(8,128)(2,1)S(1)}, bf16[144,1408]{1,0:T(8,128)(2,1)S(1)}, u32[]{:S(2)}, u32[]{:S(2)}) collective-permute-start(bf16[144,1408]{1,0:T(8,128)(2,1)S(1)} %get-tuple-element.141), channel_id=1, source_target_pairs={{12,0},{18,6},{24,12},{30,18},{36,24},{42,30},{48,36},{54,42},{60,... | collective-permute-start | bytes 1216520 | tf_op jit(solution)/shard_map/cond/branch_2_fun/ppermute | solution.py:21
  64.9 37.3 %collective-permute-start.34 = (bf16[72,4096]{1,0:T(8,128)(2,1)S(1)}, bf16[72,4096]{1,0:T(8,128)(2,1)}, u32[]{:S(2)}, u32[]{:S(2)}) collective-permute-start(bf16[72,4096]{1,0:T(8,128)(2,1)S(1)} %bitcast.118), channel_id=1, source_target_pairs={{0,1},{1,0},{2,3},{3,2},{4,5},{5,4},{6,7},{7,6},{8,9},{9,8},{10,11... | collective-permute-start | bytes 1769480 | tf_op jit(solution)/shard_map/cond/branch_2_fun/ppermute | solution.py:25
  121.3 24.9 %collective-permute-start.38 = (bf16[72,4096]{1,0:T(8,128)(2,1)S(1)}, bf16[72,4096]{1,0:T(8,128)(2,1)}, u32[]{:S(2)}, u32[]{:S(2)}) collective-permute-start(bf16[72,4096]{1,0:T(8,128)(2,1)S(1)} %slice.127), channel_id=1, source_target_pairs={{0,1},{1,0},{2,3},{3,2},{4,5},{5,4},{6,7},{7,6},{8,9},{9,8},{10,11... | collective-permute-start | bytes 1769480 | tf_op jit(solution)/shard_map/ppermute | solution.py:25
  125.0 12.7 %all-to-all-start.1 = ((f32[24,8,128]{2,1,0:T(8,128)}), f32[24,8,128]{2,1,0:T(8,128)S(1)}, u32[]{:S(2)}, u32[]{:S(2)}) async-start(f32[24,8,128]{2,1,0:T(8,128)} %maximum_maximum_fusion), calls=%async_computation.1 | async-start | bytes 196608 | tf_op jit(solution)/shard_map/all_to_all | solution.py:130
  131.7 34.3 %copy-start.2 = (bf16[24,4096]{1,0:T(8,128)(2,1)S(1)}, bf16[24,4096]{1,0:T(8,128)(2,1)}, u32[]{:S(2)}) copy-start(bf16[24,4096]{1,0:T(8,128)(2,1)} %param.43) | copy-start | bytes 589828
  138.5 21.5 %all-to-all-start.2 = ((f32[32,8,128]{2,1,0:T(8,128)}), f32[32,8,128]{2,1,0:T(8,128)S(1)}, u32[]{:S(2)}, u32[]{:S(2)}) async-start(f32[32,8,128]{2,1,0:T(8,128)} %broadcast_in_dim.39), calls=%async_computation.2 | async-start | bytes 262144 | tf_op jit(solution)/shard_map/all_to_all | solution.py:30
  147.4 1.0 copy-start.1
  148.5 17.4 %collective-permute-start.39 = (bf16[24,4096]{1,0:T(8,128)(2,1)S(1)}, bf16[24,4096]{1,0:T(8,128)(2,1)S(1)}, u32[]{:S(2)}, u32[]{:S(2)}) collective-permute-start(bf16[24,4096]{1,0:T(8,128)(2,1)S(1)} %get-tuple-element.185), channel_id=1, source_target_pairs={{0,2},{2,4},{4,0},{1,3},{3,5},{5,1},{6,8},{8,10},{10,6},{7,9},{9,1... | collective-permute-start | bytes 589832 | tf_op jit(solution)/shard_map/ppermute | solution.py:101
  150.4 15.5 %collective-permute-start.40 = (bf16[24,4096]{1,0:T(8,128)(2,1)S(1)}, bf16[24,4096]{1,0:T(8,128)(2,1)S(1)}, u32[]{:S(2)}, u32[]{:S(2)}) collective-permute-start(bf16[24,4096]{1,0:T(8,128)(2,1)S(1)} %get-tuple-element.186), channel_id=1, source_target_pairs={{0,4},{2,0},{4,2},{1,5},{3,1},{5,3},{6,10},{8,6},{10,8},{7,11},{9,... | collective-permute-start | bytes 589832 | tf_op jit(solution)/shard_map/ppermute | solution.py:101
  160.6 12.5 %all-to-all-start.3 = ((f32[24,8,128]{2,1,0:T(8,128)}), f32[24,8,128]{2,1,0:T(8,128)S(1)}, u32[]{:S(2)}, u32[]{:S(2)}) async-start(f32[24,8,128]{2,1,0:T(8,128)} %broadcast_in_dim.40), calls=%async_computation.3 | async-start | bytes 196608 | tf_op jit(solution)/shard_map/all_to_all | solution.py:30
where the time goes:
time: 176 us; the launch traced here: 175 us
  starting transfers between devices  76 us (43%)
  waiting for transfers between devices  64.7 us (37%)
  matrix products  14.8 us (8%)
  other arithmetic  9.69 us (6%)
  local copies, waits for them, and re-layouts  6.8 us (4%)
    ppermute x2, waiting for transfers between devices, pull(): lax.ppermute(value, DP, [((i + steps) % N_DP, i) for i in range(N_DP)])  49.5 us
    ppermute x2, starting transfers between devices, pull(): lax.ppermute(value, DP, [((i + steps) % N_DP, i) for i in range(N_DP)])  33.9 us
    all_to_all x3, starting transfers between devices, spread(): return lax.all_to_all(copies, axes, 0, 0, tiled=True)  19 us
    ppermute x2, starting transfers between devices, swap_cores(): return lax.ppermute(value, 'c', [(0, 1), (1, 0)])  11.4 us
    all_to_all x3, waiting for transfers between devices, spread(): return lax.all_to_all(copies, axes, 0, 0, tiled=True)  9.31 us
    dot_general x1, matrix products, shards(): lax.dot_general(grad_out, projection, (((1,), (1,)), ((), ())), preferred...  8.21 us
    dot_general x1, matrix products, branch(): jnp.dot(rows, projection, preferred_element_type=jnp.float32) + bias  6.56 us
    ppermute x2, starting transfers between devices, shards(): piece = lax.ppermute(piece.astype(jnp.bfloat16), 'zl', ring)  6.18 us
  transfers between devices with their start and end apart: 10, of which 5 were waited for; matrix products, arithmetic and copies ran while one was open for 5% of the time, Pallas kernels for 0%

commit v1 on v0

--- a/solution.py
+++ b/solution.py
@@ -2,6 +2,7 @@
 import jax.numpy as jnp
 import numpy as np
 from jax import lax
+from jax.experimental import pallas as pl
 from jax.sharding import Mesh, PartitionSpec as P
 
 
@@ -15,6 +16,8 @@
 N_X, N_Y, N_ZH, N_ZL, N_C = SIZES
 N_DP = N_X * N_Y * N_ZH
 LANES = 128
+BLOCK = 512
+INTERPRET = False
 
 
 def pull(value, steps):
@@ -42,6 +45,57 @@
     entries = rows.astype(jnp.float32)
     inverse = lax.rsqrt(jnp.mean(entries * entries, axis=-1, keepdims=True) + NORM_EPS)
     return entries * inverse, inverse
+
+
+def back_body(grad_ref, weights_ref, mine_ref, other_ref, inverse_ref, own_ref, far_ref, gain_ref):
+    half = mine_ref.shape[0]
+    grads = lax.dot_general(
+        grad_ref[...], weights_ref[...], (((1,), (1,)), ((), ())), preferred_element_type=jnp.float32
+    )
+    own, far = grads[:half], grads[half:]
+    own_ref[...] = own
+    far_ref[...] = far.astype(jnp.bfloat16)
+    here = own * (mine_ref[...].astype(jnp.float32) * inverse_ref[:half])
+    there = far * (other_ref[...].astype(jnp.float32) * inverse_ref[half:])
+    gain_ref[...] = jnp.sum(here + there, axis=0, keepdims=True)
+
+
+def back(grad_out, weights, mine, other, inverse):
+    rows, columns = grad_out.shape
+    half, width = mine.shape
+    block = BLOCK
+    while width % block:
+        block //= 2
+    whole = lambda i: (0, 0)
+    along = lambda i: (0, i)
+    return pl.pallas_call(
+        back_body,
+        grid=(width // block,),
+        in_specs=[
+            pl.BlockSpec((rows, columns), whole),
+            pl.BlockSpec((block, columns), lambda i: (i, 0)),
+            pl.BlockSpec((half, block), along),
+            pl.BlockSpec((half, block), along),
+            pl.BlockSpec((rows, 1), whole),
+        ],
+        out_specs=[
+            pl.BlockSpec((half, block), along),
+            pl.BlockSpec((half, block), along),
+            pl.BlockSpec((1, block), along),
+        ],
+        out_shape=[
+            jax.ShapeDtypeStruct((half, width), jnp.float32),
+            jax.ShapeDtypeStruct((half, width), jnp.bfloat16),
+            jax.ShapeDtypeStruct((1, width), jnp.float32),
+        ],
+        cost_estimate=pl.CostEstimate(
+            flops=2 * rows * columns * width,
+            bytes_accessed=2 * columns * width + 10 * half * width,
+            transcendentals=0,
+        ),
+        name="back",
+        interpret=INTERPRET,
+    )(grad_out, weights, mine, other, inverse)
 
 
 def shards(hidden, doc_ids, teacher, rotation, gain, bias, projection):
@@ -84,22 +138,19 @@
     grad_out, loss_part, bias_part, other, block_inverse = lax.switch(
         turn % N_ZH, [near(s) for s in range(N_ZH)], moved, gathered, weight
     )
-    grad_all = lax.dot_general(
-        grad_out, projection, (((1,), (1,)), ((), ())), preferred_element_type=jnp.float32
-    )
-    block = jnp.concatenate([gathered.reshape(-1, width), other], 0)
-    gain_part = jnp.sum(grad_all * (block.astype(jnp.float32) * block_inverse), axis=0) / tokens
-
-    half = block_rows // N_C
-    summed = grad_all[:half] + swap_cores(grad_all[half:].astype(jnp.bfloat16)).astype(jnp.float32)
+    own_rows, far_rows, gain_part = back(
+        grad_out, projection, gathered.reshape(-1, width), other, block_inverse
+    )
+    gain_part = gain_part / tokens
+    summed = own_rows + swap_cores(far_rows).astype(jnp.float32)
     summed = summed.reshape(N_ZL, portion_rows, width)
     at = lax.axis_index("zl")
     portion_gradient = lax.dynamic_index_in_dim(summed, at, 0, keepdims=False)
+    pieces = []
     for step in range(1, N_ZL):
         piece = lax.dynamic_index_in_dim(summed, (at + step) % N_ZL, 0, keepdims=False)
         ring = [(i, (i + step) % N_ZL) for i in range(N_ZL)]
-        piece = lax.ppermute(piece.astype(jnp.bfloat16), "zl", ring)
-        portion_gradient = portion_gradient + piece.astype(jnp.float32)
+        pieces.append(lax.ppermute(piece.astype(jnp.bfloat16), "zl", ring))
 
     n_tensor = N_ZL * N_C
     peers = N_X * n_tensor
@@ -142,6 +193,8 @@
     grad_bias = by_x.reshape(N_X * bias_each, LANES)[:bias_lines].reshape(columns)
 
     unscaled, inverse = normalized(hidden)
+    for piece in pieces:
+        portion_gradient = portion_gradient + piece.astype(jnp.float32)
     unscaled_gradient = portion_gradient * gain
     inner = jnp.mean(unscaled_gradient * unscaled, axis=-1, keepdims=True)
     hidden_gradient = (inverse * (unscaled_gradient - unscaled * inner)).astype(jnp.bfloat16)

time: 176 us -> 178 us (1.011)
  Pallas kernels: 0 us -> 9.91 us
  matrix products: 14.8 us -> 6.55 us
  waiting for transfers between devices: 64.7 us -> 68.5 us
  other arithmetic: 9.69 us -> 7.13 us
    pallas_call x0 -> x1, Pallas kernels: none -> 9.91 us  [back(): pl.pallas_call(back_body, grid=(width // block,), in_specs=[pl.BlockSpec(...]
    dot_general x1 -> x0, matrix products: 8.21 us -> none  [shards(): lax.dot_general(grad_out, projection, (((1,), (1,)), ((), ())), preferred...]
    all_to_all x3, waiting for transfers between devices: 9.31 us -> 12.1 us  [spread(): return lax.all_to_all(copies, axes, 0, 0, tiled=True)]
  transfers between devices with their start and end apart: 10 -> 10, of which waited for: 5 -> 5; matrix products, arithmetic and copies ran while one was open for 5% -> 3% of each run, Pallas kernels for 0% -> 0%
where the time goes in v1:
time: 178 us; the launch traced here: 177 us
  starting transfers between devices  76 us (43%)
  waiting for transfers between devices  68.5 us (38%)
  Pallas kernels  9.91 us (6%)
  other arithmetic  7.13 us (4%)
  matrix products  6.55 us (4%)
  local copies, waits for them, and re-layouts  5.83 us (3%)
    ppermute x2, waiting for transfers between devices, pull(): lax.ppermute(value, DP, [((i + steps) % N_DP, i) for i in range(N_DP)])  49.5 us
    ppermute x2, starting transfers between devices, pull(): lax.ppermute(value, DP, [((i + steps) % N_DP, i) for i in range(N_DP)])  33.9 us
    all_to_all x3, starting transfers between devices, spread(): return lax.all_to_all(copies, axes, 0, 0, tiled=True)  19 us
    all_to_all x3, waiting for transfers between devices, spread(): return lax.all_to_all(copies, axes, 0, 0, tiled=True)  12.1 us
    ppermute x2, starting transfers between devices, swap_cores(): return lax.ppermute(value, 'c', [(0, 1), (1, 0)])  11.3 us
    pallas_call x1, Pallas kernels, back(): pl.pallas_call(back_body, grid=(width // block,), in_specs=[pl.BlockSpec(...  9.91 us
    all_to_all x1, waiting for transfers between devices, shards(): lines = lax.all_to_all(lines, group, 0, 0, tiled=True)  6.86 us
    dot_general x1, matrix products, branch(): jnp.dot(rows, projection, preferred_element_type=jnp.float32) + bias  6.55 us
  transfers between devices with their start and end apart: 10, of which 5 were waited for; matrix products, arithmetic and copies ran while one was open for 3% of the time, Pallas kernels for 0%

profile of v1, /device:TPU:1, one launch (start us, length us, event | category | flops | bytes accessed | tf_op | source)
XLA Modules:
  0.0 176.8 jit_solution(14647989199379087382)
XLA Ops:
  0.6 0.0 copy-start
  0.6 0.0 copy-start.2
  0.7 1.9 %broadcast_in_dim.31 = bf16[3,24,4096]{2,1,0:T(8,128)(2,1)} broadcast(bf16[24,4096]{1,0:T(8,128)(2,1)} %param.43), dimensions={1,2} | broadcast | bytes 786432 | tf_op jit(solution)/shard_map/broadcast_in_dim | solution.py:32
  2.5 6.0 %all-to-all-start = ((bf16[3,24,4096]{2,1,0:T(8,128)(2,1)}), bf16[3,24,4096]{2,1,0:T(8,128)(2,1)S(1)}, u32[]{:S(2)}, u32[]{:S(2)}) async-start(bf16[3,24,4096]{2,1,0:T(8,128)(2,1)} %broadcast_in_dim.31), calls=%async_computation | async-start | bytes 1179648 | tf_op jit(solution)/shard_map/all_to_all | solution.py:33
  9.2 0.0 copy-done
  9.2 0.2 dynamic-slice_reduce_fusion
  9.4 0.2 convert_reduce_fusion.4
  9.6 0.1 div.75
  9.7 0.1 select_n.154
  9.8 0.1 select_n.156
  9.9 0.1 pad.26.clone
  10.0 0.1 pad.23.clone
  10.1 0.0 copy-done.2
  10.1 0.0 copy-start.3
  10.1 0.0 copy-start.4
  10.1 27.4 %conditional.2 = (bf16[144,1408]{1,0:T(8,128)(2,1)S(1)}) conditional(s32[]{:T(128)} %clamp.7, bf16[144,1408]{1,0:T(8,128)(2,1)S(1)} %copy-done.2, bf16[144,1408]{1,0:T(8,128)(2,1)S(1)} %copy-done.2, bf16[144,1408]{1,0:T(8,128)(2,1)S(1)} %copy-done.2, bf16[144,1408]{1,0:T(8,128)(2,1)S(1)} %copy-done.2, ...), branch_computations={%region_1.2_spmd, %region_2.3_spmd, %region_3.4_spmd, %region_4.5_... | conditional | bytes 2433072 | solution.py:114
  10.1 6.7 %collective-permute-start.26 = (bf16[144,1408]{1,0:T(8,128)(2,1)S(1)}, bf16[144,1408]{1,0:T(8,128)(2,1)S(1)}, u32[]{:S(2)}, u32[]{:S(2)}) collective-permute-start(bf16[144,1408]{1,0:T(8,128)(2,1)S(1)} %param.27), channel_id=1, source_target_pairs={{648,0},{654,6},{660,12},{666,18},{672,24},{678,30},{684,36},{690,... | collective-permute-start | bytes 1216520 | tf_op jit(solution)/shard_map/cond/branch_27_fun/ppermute | solution.py:24
  16.8 20.7 %collective-permute-done.26 = bf16[144,1408]{1,0:T(8,128)(2,1)S(1)} collective-permute-done((bf16[144,1408]{1,0:T(8,128)(2,1)S(1)}, bf16[144,1408]{1,0:T(8,128)(2,1)S(1)}, u32[]{:S(2)}, u32[]{:S(2)}) %collective-permute-start.26) | collective-permute-done | bytes 405536 | tf_op jit(solution)/shard_map/cond/branch_27_fun/ppermute | solution.py:24
  37.5 0.1 pad_maximum_fusion.12
  37.6 0.0 all-to-all-done
  37.6 0.0 copy-done.3
  37.6 0.0 copy-done.4
  37.6 74.8 %conditional.3 = (bf16[144,1408]{1,0:T(8,128)(2,1)S(1)}, f32[]{:T(128)}, f32[1408]{0:T(1024)S(1)}, bf16[72,4096]{1,0:T(8,128)(2,1)}, f32[144,1]{1,0:T(8,128)S(1)}) conditional(s32[]{:T(128)} %clamp.6, (f32[144,1]{0,1:T(1,128)S(1)}, bf16[3,24,4096]{2,1,0:T(8,128)(2,1)S(1)}, f32[4096]{0:T(1024)S(1)}, ...), branch_computations={%region_34.0_spmd, %region_38.42_spmd, %region_42.46_spmd, %region... | conditional | flops 1671248000 | bytes 21162064 | solution.py:138
  37.6 27.3 %collective-permute-start.35 = (bf16[144,1408]{1,0:T(8,128)(2,1)S(1)}, bf16[144,1408]{1,0:T(8,128)(2,1)S(1)}, u32[]{:S(2)}, u32[]{:S(2)}) collective-permute-start(bf16[144,1408]{1,0:T(8,128)(2,1)S(1)} %get-tuple-element.141), channel_id=1, source_target_pairs={{12,0},{18,6},{24,12},{30,18},{36,24},{42,30},{48,36},{54,42},{60,... | collective-permute-start | bytes 1216520 | tf_op jit(solution)/shard_map/cond/branch_2_fun/ppermute | solution.py:24
  64.9 8.5 %collective-permute-start.34 = (bf16[72,4096]{1,0:T(8,128)(2,1)S(1)}, bf16[72,4096]{1,0:T(8,128)(2,1)}, u32[]{:S(2)}, u32[]{:S(2)}) collective-permute-start(bf16[72,4096]{1,0:T(8,128)(2,1)S(1)} %bitcast.114), channel_id=1, source_target_pairs={{0,1},{1,0},{2,3},{3,2},{4,5},{5,4},{6,7},{7,6},{8,9},{9,8},{10,11... | collective-permute-start | bytes 1769480 | tf_op jit(solution)/shard_map/cond/branch_2_fun/ppermute | solution.py:28
  73.4 28.8 %collective-permute-done.35 = bf16[144,1408]{1,0:T(8,128)(2,1)S(1)} collective-permute-done((bf16[144,1408]{1,0:T(8,128)(2,1)S(1)}, bf16[144,1408]{1,0:T(8,128)(2,1)S(1)}, u32[]{:S(2)}, u32[]{:S(2)}) %collective-permute-start.35) | collective-permute-done | bytes 405536 | tf_op jit(solution)/shard_map/cond/branch_2_fun/ppermute | solution.py:24
  102.2 0.0 collective-permute-done.34
  102.2 1.4 fusion.16
  103.6 6.6 %convolution_add_fusion.2 = f32[144,1408]{1,0:T(8,128)S(1)} fusion(bf16[4096,1408]{1,0:T(8,128)(2,1)} %get-tuple-element.138, f32[4096]{0:T(1024)S(1)} %get-tuple-element.137, f32[144]{0:T(256)S(1)} %add_rsqrt_fusion.2, bf16[72,4096]{1,0:T(8,128)(2,1)} %collective-permute-done.34, bf16[72,4096]{1,0:T(8,128)(2,1)S(1)} %bitcast.116, ...), kind=kOutput, calls=%fused_computation.46 | convolution fusion | flops 1665275904 | bytes 13547584 | tf_op jit(solution)/shard_map/cond/branch_2_fun/dot_general | solution.py:128
  110.2 1.0 convert_reduce_fusion.2
  111.8 0.1 copy.63
  112.4 0.0 copy-start.1
  112.5 9.9 %back.1 = (f32[72,4096]{1,0:T(8,128)}, bf16[72,4096]{1,0:T(8,128)(2,1)}, f32[1,4096]{1,0:T(1,128)}) custom-call(bf16[144,1408]{1,0:T(8,128)(2,1)S(1)} %get-tuple-element.161.grad_ref, bf16[4096,1408]{1,0:T(8,128)(2,1)} %weights_ref.1, bf16[72,4096]{1,0:T(8,128)(2,1)S(1)} %bitcast.107, bf16[72,4096]{1,0:T(8,128)(2,1)} %get-tuple-element.162.other_ref, ...), custom_call_target="tpu_custom_call" | custom-call | flops 1660944384 | bytes 14483456 | tf_op jit(solution)/shard_map/back/pallas_call | solution.py:71
  122.4 0.7 broadcast_multiply_fusion.4
  123.1 0.1 pad.25.clone
  123.2 2.9 %collective-permute-start.38 = (bf16[72,4096]{1,0:T(8,128)(2,1)}, bf16[72,4096]{1,0:T(8,128)(2,1)S(1)}, u32[]{:S(2)}, u32[]{:S(2)}) collective-permute-start(bf16[72,4096]{1,0:T(8,128)(2,1)} %get-tuple-element.165), channel_id=1, source_target_pairs={{0,1},{1,0},{2,3},{3,2},{4,5},{5,4},{6,7},{7,6},{8,9},{9,8},{10,11... | collective-permute-start | bytes 1769480 | tf_op jit(solution)/shard_map/ppermute | solution.py:28
  126.1 0.1 maximum_maximum_fusion.1
  126.2 0.7 maximum_maximum_fusion
  126.9 5.5 %all-to-all-start.1 = ((f32[24,8,128]{2,1,0:T(8,128)}), f32[24,8,128]{2,1,0:T(8,128)S(1)}, u32[]{:S(2)}, u32[]{:S(2)}) async-start(f32[24,8,128]{2,1,0:T(8,128)} %maximum_maximum_fusion), calls=%async_computation.1 | async-start | bytes 196608 | tf_op jit(solution)/shard_map/all_to_all | solution.py:181
  132.5 0.0 copy-done.1
  132.5 0.2 fusion.38
  132.7 6.9 %all-to-all-done.1 = f32[24,8,128]{2,1,0:T(8,128)S(1)} async-done(((f32[24,8,128]{2,1,0:T(8,128)}), f32[24,8,128]{2,1,0:T(8,128)S(1)}, u32[]{:S(2)}, u32[]{:S(2)}) %all-to-all-start.1) | async-done | bytes 98336 | tf_op jit(solution)/shard_map/all_to_all | solution.py:181
  139.5 0.1 select_reduce_fusion
  139.7 0.7 broadcast_in_dim.39
  140.3 7.8 %all-to-all-start.2 = ((f32[32,8,128]{2,1,0:T(8,128)}), f32[32,8,128]{2,1,0:T(8,128)S(1)}, u32[]{:S(2)}, u32[]{:S(2)}) async-start(f32[32,8,128]{2,1,0:T(8,128)} %broadcast_in_dim.39), calls=%async_computation.2 | async-start | bytes 262144 | tf_op jit(solution)/shard_map/all_to_all | solution.py:33
  148.1 0.0 collective-permute-done.38
  148.1 1.4 convert_add_fusion
  149.5 0.1 fusion.41
  149.6 1.9 %collective-permute-start.39 = (bf16[24,4096]{1,0:T(8,128)(2,1)S(1)}, bf16[24,4096]{1,0:T(8,128)(2,1)S(1)}, u32[]{:S(2)}, u32[]{:S(2)}) collective-permute-start(bf16[24,4096]{1,0:T(8,128)(2,1)S(1)} %get-tuple-element.212), channel_id=1, source_target_pairs={{0,2},{2,4},{4,0},{1,3},{3,5},{5,1},{6,8},{8,10},{10,6},{7,9},{9,1... | collective-permute-start | bytes 589832 | tf_op jit(solution)/shard_map/ppermute | solution.py:153
  151.5 4.3 %collective-permute-start.40 = (bf16[24,4096]{1,0:T(8,128)(2,1)S(1)}, bf16[24,4096]{1,0:T(8,128)(2,1)S(1)}, u32[]{:S(2)}, u32[]{:S(2)}) collective-permute-start(bf16[24,4096]{1,0:T(8,128)(2,1)S(1)} %get-tuple-element.213), channel_id=1, source_target_pairs={{0,4},{2,0},{4,2},{1,5},{3,1},{5,3},{6,10},{8,6},{10,8},{7,11},{9,... | collective-permute-start | bytes 589832 | tf_op jit(solution)/shard_map/ppermute | solution.py:153
  155.8 6.0 %all-to-all-done.2 = f32[32,8,128]{2,1,0:T(8,128)S(1)} async-done(((f32[32,8,128]{2,1,0:T(8,128)}), f32[32,8,128]{2,1,0:T(8,128)S(1)}, u32[]{:S(2)}, u32[]{:S(2)}) %all-to-all-start.2) | async-done | bytes 131104 | tf_op jit(solution)/shard_map/all_to_all | solution.py:33
  161.9 0.6 broadcast_in_dim.40
  162.5 5.2 %all-to-all-start.3 = ((f32[24,8,128]{2,1,0:T(8,128)}), f32[24,8,128]{2,1,0:T(8,128)S(1)}, u32[]{:S(2)}, u32[]{:S(2)}) async-start(f32[24,8,128]{2,1,0:T(8,128)} %broadcast_in_dim.40), calls=%async_computation.3 | async-start | bytes 196608 | tf_op jit(solution)/shard_map/all_to_all | solution.py:33
  167.8 0.0 collective-permute-done.39
  167.8 0.0 collective-permute-done.40
  167.8 0.2 fusion.34
  168.1 0.8 fusion.37
  168.9 6.1 %all-to-all-done.3 = f32[24,8,128]{2,1,0:T(8,128)S(1)} async-done(((f32[24,8,128]{2,1,0:T(8,128)}), f32[24,8,128]{2,1,0:T(8,128)S(1)}, u32[]{:S(2)}, u32[]{:S(2)}) %all-to-all-start.3) | async-done | bytes 98336 | tf_op jit(solution)/shard_map/all_to_all | solution.py:33
  175.0 0.6 slice_bitcast_fusion.8
  175.7 0.5 slice.68
  176.2 0.6 slice.64
  (21 shorter events, 0.3 us)
Async XLA Ops:
  0.6 8.6 %copy-start = (s32[128,144]{0,1:T(8,128)S(1)}, s32[128,144]{0,1:T(8,128)}, u32[]{:S(2)}) copy-start(s32[128,144]{0,1:T(8,128)} %param.44) | copy-start | bytes 221188
  0.6 9.4 %copy-start.2 = (bf16[144,1408]{1,0:T(8,128)(2,1)S(1)}, bf16[144,1408]{1,0:T(8,128)(2,1)}, u32[]{:S(2)}) copy-start(bf16[144,1408]{1,0:T(8,128)(2,1)} %param.45) | copy-start | bytes 1216516
  2.5 35.1 %all-to-all-start = ((bf16[3,24,4096]{2,1,0:T(8,128)(2,1)}), bf16[3,24,4096]{2,1,0:T(8,128)(2,1)S(1)}, u32[]{:S(2)}, u32[]{:S(2)}) async-start(bf16[3,24,4096]{2,1,0:T(8,128)(2,1)} %broadcast_in_dim.31), calls=%async_computation | async-start | bytes 1179648 | tf_op jit(solution)/shard_map/all_to_all | solution.py:33
  10.1 27.5 %copy-start.3 = (f32[4096]{0:T(1024)S(1)}, f32[4096]{0:T(1024)}, u32[]{:S(2)}) copy-start(f32[4096]{0:T(1024)} %param.47) | copy-start | bytes 49156
  10.1 27.5 %copy-start.4 = (f32[1408]{0:T(1024)S(1)}, f32[1408]{0:T(1024)}, u32[]{:S(2)}) copy-start(f32[1408]{0:T(1024)} %param.48) | copy-start | bytes 16900
  10.1 27.4 %collective-permute-start.26 = (bf16[144,1408]{1,0:T(8,128)(2,1)S(1)}, bf16[144,1408]{1,0:T(8,128)(2,1)S(1)}, u32[]{:S(2)}, u32[]{:S(2)}) collective-permute-start(bf16[144,1408]{1,0:T(8,128)(2,1)S(1)} %param.27), channel_id=1, source_target_pairs={{648,0},{654,6},{660,12},{666,18},{672,24},{678,30},{684,36},{690,... | collective-permute-start | bytes 1216520 | tf_op jit(solution)/shard_map/cond/branch_27_fun/ppermute | solution.py:24
  37.6 64.6 %collective-permute-start.35 = (bf16[144,1408]{1,0:T(8,128)(2,1)S(1)}, bf16[144,1408]{1,0:T(8,128)(2,1)S(1)}, u32[]{:S(2)}, u32[]{:S(2)}) collective-permute-start(bf16[144,1408]{1,0:T(8,128)(2,1)S(1)} %get-tuple-element.141), channel_id=1, source_target_pairs={{12,0},{18,6},{24,12},{30,18},{36,24},{42,30},{48,36},{54,42},{60,... | collective-permute-start | bytes 1216520 | tf_op jit(solution)/shard_map/cond/branch_2_fun/ppermute | solution.py:24
  64.9 37.3 %collective-permute-start.34 = (bf16[72,4096]{1,0:T(8,128)(2,1)S(1)}, bf16[72,4096]{1,0:T(8,128)(2,1)}, u32[]{:S(2)}, u32[]{:S(2)}) collective-permute-start(bf16[72,4096]{1,0:T(8,128)(2,1)S(1)} %bitcast.114), channel_id=1, source_target_pairs={{0,1},{1,0},{2,3},{3,2},{4,5},{5,4},{6,7},{7,6},{8,9},{9,8},{10,11... | collective-permute-start | bytes 1769480 | tf_op jit(solution)/shard_map/cond/branch_2_fun/ppermute | solution.py:28
  112.4 20.1 %copy-start.1 = (bf16[24,4096]{1,0:T(8,128)(2,1)S(1)}, bf16[24,4096]{1,0:T(8,128)(2,1)}, u32[]{:S(2)}) copy-start(bf16[24,4096]{1,0:T(8,128)(2,1)} %param.43) | copy-start | bytes 589828
  123.2 24.9 %collective-permute-start.38 = (bf16[72,4096]{1,0:T(8,128)(2,1)}, bf16[72,4096]{1,0:T(8,128)(2,1)S(1)}, u32[]{:S(2)}, u32[]{:S(2)}) collective-permute-start(bf16[72,4096]{1,0:T(8,128)(2,1)} %get-tuple-element.165), channel_id=1, source_target_pairs={{0,1},{1,0},{2,3},{3,2},{4,5},{5,4},{6,7},{7,6},{8,9},{9,8},{10,11... | collective-permute-start | bytes 1769480 | tf_op jit(solution)/shard_map/ppermute | solution.py:28
  126.9 12.7 %all-to-all-start.1 = ((f32[24,8,128]{2,1,0:T(8,128)}), f32[24,8,128]{2,1,0:T(8,128)S(1)}, u32[]{:S(2)}, u32[]{:S(2)}) async-start(f32[24,8,128]{2,1,0:T(8,128)} %maximum_maximum_fusion), calls=%async_computation.1 | async-start | bytes 196608 | tf_op jit(solution)/shard_map/all_to_all | solution.py:181
  140.3 21.5 %all-to-all-start.2 = ((f32[32,8,128]{2,1,0:T(8,128)}), f32[32,8,128]{2,1,0:T(8,128)S(1)}, u32[]{:S(2)}, u32[]{:S(2)}) async-start(f32[32,8,128]{2,1,0:T(8,128)} %broadcast_in_dim.39), calls=%async_computation.2 | async-start | bytes 262144 | tf_op jit(solution)/shard_map/all_to_all | solution.py:33
  149.6 18.2 %collective-permute-start.39 = (bf16[24,4096]{1,0:T(8,128)(2,1)S(1)}, bf16[24,4096]{1,0:T(8,128)(2,1)S(1)}, u32[]{:S(2)}, u32[]{:S(2)}) collective-permute-start(bf16[24,4096]{1,0:T(8,128)(2,1)S(1)} %get-tuple-element.212), channel_id=1, source_target_pairs={{0,2},{2,4},{4,0},{1,3},{3,5},{5,1},{6,8},{8,10},{10,6},{7,9},{9,1... | collective-permute-start | bytes 589832 | tf_op jit(solution)/shard_map/ppermute | solution.py:153
  151.5 16.3 %collective-permute-start.40 = (bf16[24,4096]{1,0:T(8,128)(2,1)S(1)}, bf16[24,4096]{1,0:T(8,128)(2,1)S(1)}, u32[]{:S(2)}, u32[]{:S(2)}) collective-permute-start(bf16[24,4096]{1,0:T(8,128)(2,1)S(1)} %get-tuple-element.213), channel_id=1, source_target_pairs={{0,4},{2,0},{4,2},{1,5},{3,1},{5,3},{6,10},{8,6},{10,8},{7,11},{9,... | collective-permute-start | bytes 589832 | tf_op jit(solution)/shard_map/ppermute | solution.py:153
  162.5 12.5 %all-to-all-start.3 = ((f32[24,8,128]{2,1,0:T(8,128)}), f32[24,8,128]{2,1,0:T(8,128)S(1)}, u32[]{:S(2)}, u32[]{:S(2)}) async-start(f32[24,8,128]{2,1,0:T(8,128)} %broadcast_in_dim.40), calls=%async_computation.3 | async-start | bytes 196608 | tf_op jit(solution)/shard_map/all_to_all | solution.py:33

commit v2 on v0

--- a/solution.py
+++ b/solution.py
@@ -87,19 +87,20 @@
     grad_all = lax.dot_general(
         grad_out, projection, (((1,), (1,)), ((), ())), preferred_element_type=jnp.float32
     )
+    grad_all = lax.optimization_barrier(grad_all)
     block = jnp.concatenate([gathered.reshape(-1, width), other], 0)
     gain_part = jnp.sum(grad_all * (block.astype(jnp.float32) * block_inverse), axis=0) / tokens
-
     half = block_rows // N_C
-    summed = grad_all[:half] + swap_cores(grad_all[half:].astype(jnp.bfloat16)).astype(jnp.float32)
+    own_rows, far_rows = grad_all[:half], grad_all[half:].astype(jnp.bfloat16)
+    summed = own_rows + swap_cores(far_rows).astype(jnp.float32)
     summed = summed.reshape(N_ZL, portion_rows, width)
     at = lax.axis_index("zl")
     portion_gradient = lax.dynamic_index_in_dim(summed, at, 0, keepdims=False)
+    pieces = []
     for step in range(1, N_ZL):
         piece = lax.dynamic_index_in_dim(summed, (at + step) % N_ZL, 0, keepdims=False)
         ring = [(i, (i + step) % N_ZL) for i in range(N_ZL)]
-        piece = lax.ppermute(piece.astype(jnp.bfloat16), "zl", ring)
-        portion_gradient = portion_gradient + piece.astype(jnp.float32)
+        pieces.append(lax.ppermute(piece.astype(jnp.bfloat16), "zl", ring))
 
     n_tensor = N_ZL * N_C
     peers = N_X * n_tensor
@@ -142,6 +143,8 @@
     grad_bias = by_x.reshape(N_X * bias_each, LANES)[:bias_lines].reshape(columns)
 
     unscaled, inverse = normalized(hidden)
+    for piece in pieces:
+        portion_gradient = portion_gradient + piece.astype(jnp.float32)
     unscaled_gradient = portion_gradient * gain
     inner = jnp.mean(unscaled_gradient * unscaled, axis=-1, keepdims=True)
     hidden_gradient = (inverse * (unscaled_gradient - unscaled * inner)).astype(jnp.bfloat16)

time: 176 us -> 178 us (1.011)
  waiting for transfers between devices: 64.7 us -> 66.7 us
  transfers between devices with their start and end apart: 10 -> 10, of which waited for: 5 -> 5; matrix products, arithmetic and copies ran while one was open for 5% -> 4% of each run, Pallas kernels for 0% -> 0%
where the time goes in v2:
time: 178 us; the launch traced here: 177 us
  starting transfers between devices  76 us (43%)
  waiting for transfers between devices  66.7 us (37%)
  matrix products  14.7 us (8%)
  other arithmetic  9.23 us (5%)
  local copies, waits for them, and re-layouts  7.61 us (4%)
    ppermute x2, waiting for transfers between devices, pull(): lax.ppermute(value, DP, [((i + steps) % N_DP, i) for i in range(N_DP)])  49.5 us
    ppermute x2, starting transfers between devices, pull(): lax.ppermute(value, DP, [((i + steps) % N_DP, i) for i in range(N_DP)])  33.9 us
    all_to_all x3, starting transfers between devices, spread(): return lax.all_to_all(copies, axes, 0, 0, tiled=True)  19 us
    ppermute x2, starting transfers between devices, swap_cores(): return lax.ppermute(value, 'c', [(0, 1), (1, 0)])  11.3 us
    all_to_all x3, waiting for transfers between devices, spread(): return lax.all_to_all(copies, axes, 0, 0, tiled=True)  10.4 us
    dot_general x1, matrix products, shards(): lax.dot_general(grad_out, projection, (((1,), (1,)), ((), ())), preferred...  8.12 us
    all_to_all x1, waiting for transfers between devices, shards(): lines = lax.all_to_all(lines, group, 0, 0, tiled=True)  6.86 us
    dot_general x1, matrix products, branch(): jnp.dot(rows, projection, preferred_element_type=jnp.float32) + bias  6.57 us
  transfers between devices with their start and end apart: 10, of which 5 were waited for; matrix products, arithmetic and copies ran while one was open for 4% of the time, Pallas kernels for 0%

profile of v2, /device:TPU:1, one launch (start us, length us, event | category | flops | bytes accessed | tf_op | source)
XLA Modules:
  0.0 177.2 jit_solution(6217561191916631826)
XLA Ops:
  0.6 0.0 copy-start
  0.6 0.0 copy-start.3
  0.7 1.8 %broadcast_in_dim.31 = bf16[3,24,4096]{2,1,0:T(8,128)(2,1)} broadcast(bf16[24,4096]{1,0:T(8,128)(2,1)} %param.43), dimensions={1,2} | broadcast | bytes 786432 | tf_op jit(solution)/shard_map/broadcast_in_dim | solution.py:29
  2.5 6.0 %all-to-all-start = ((bf16[3,24,4096]{2,1,0:T(8,128)(2,1)}), bf16[3,24,4096]{2,1,0:T(8,128)(2,1)S(1)}, u32[]{:S(2)}, u32[]{:S(2)}) async-start(bf16[3,24,4096]{2,1,0:T(8,128)(2,1)} %broadcast_in_dim.31), calls=%async_computation | async-start | bytes 1179648 | tf_op jit(solution)/shard_map/all_to_all | solution.py:30
  9.2 0.0 copy-done
  9.2 0.2 dynamic-slice_reduce_fusion
  9.4 0.2 convert_reduce_fusion.4
  9.6 0.1 div.77
  9.7 0.1 select_n.154
  9.8 0.1 select_n.156
  9.9 0.1 pad.26.clone
  10.0 0.1 pad.23.clone
  10.1 0.0 copy-done.3
  10.1 0.0 copy-start.4
  10.1 0.0 copy-start.5
  10.1 27.4 %conditional.2 = (bf16[144,1408]{1,0:T(8,128)(2,1)S(1)}) conditional(s32[]{:T(128)} %clamp.7, bf16[144,1408]{1,0:T(8,128)(2,1)S(1)} %copy-done.3, bf16[144,1408]{1,0:T(8,128)(2,1)S(1)} %copy-done.3, bf16[144,1408]{1,0:T(8,128)(2,1)S(1)} %copy-done.3, bf16[144,1408]{1,0:T(8,128)(2,1)S(1)} %copy-done.3, ...), branch_computations={%region_1.2_spmd, %region_2.3_spmd, %region_3.4_spmd, %region_4.5_... | conditional | bytes 2433072 | solution.py:60
  10.1 6.7 %collective-permute-start.26 = (bf16[144,1408]{1,0:T(8,128)(2,1)S(1)}, bf16[144,1408]{1,0:T(8,128)(2,1)S(1)}, u32[]{:S(2)}, u32[]{:S(2)}) collective-permute-start(bf16[144,1408]{1,0:T(8,128)(2,1)S(1)} %param.27), channel_id=1, source_target_pairs={{648,0},{654,6},{660,12},{666,18},{672,24},{678,30},{684,36},{690,... | collective-permute-start | bytes 1216520 | tf_op jit(solution)/shard_map/cond/branch_27_fun/ppermute | solution.py:21
  16.8 20.7 %collective-permute-done.26 = bf16[144,1408]{1,0:T(8,128)(2,1)S(1)} collective-permute-done((bf16[144,1408]{1,0:T(8,128)(2,1)S(1)}, bf16[144,1408]{1,0:T(8,128)(2,1)S(1)}, u32[]{:S(2)}, u32[]{:S(2)}) %collective-permute-start.26) | collective-permute-done | bytes 405536 | tf_op jit(solution)/shard_map/cond/branch_27_fun/ppermute | solution.py:21
  37.5 0.1 pad_maximum_fusion.12
  37.6 0.0 all-to-all-done
  37.6 0.0 copy-done.4
  37.6 0.0 copy-done.5
  37.6 75.3 %conditional.3 = (bf16[144,1408]{1,0:T(8,128)(2,1)S(1)}, f32[]{:T(128)}, f32[1408]{0:T(1024)S(1)}, bf16[72,4096]{1,0:T(8,128)(2,1)}, f32[144,1]{0,1:T(1,128)}) conditional(s32[]{:T(128)} %clamp.6, (f32[144,1]{0,1:T(1,128)S(1)}, bf16[3,24,4096]{2,1,0:T(8,128)(2,1)S(1)}, f32[4096]{0:T(1024)S(1)}, ...), branch_computations={%region_34.0_spmd, %region_38.42_spmd, %region_42.46_spmd, %region... | conditional | flops 1671248000 | bytes 21160912 | solution.py:84
  37.6 27.3 %collective-permute-start.35 = (bf16[144,1408]{1,0:T(8,128)(2,1)S(1)}, bf16[144,1408]{1,0:T(8,128)(2,1)S(1)}, u32[]{:S(2)}, u32[]{:S(2)}) collective-permute-start(bf16[144,1408]{1,0:T(8,128)(2,1)S(1)} %get-tuple-element.141), channel_id=1, source_target_pairs={{12,0},{18,6},{24,12},{30,18},{36,24},{42,30},{48,36},{54,42},{60,... | collective-permute-start | bytes 1216520 | tf_op jit(solution)/shard_map/cond/branch_2_fun/ppermute | solution.py:21
  64.9 8.5 %collective-permute-start.34 = (bf16[72,4096]{1,0:T(8,128)(2,1)S(1)}, bf16[72,4096]{1,0:T(8,128)(2,1)}, u32[]{:S(2)}, u32[]{:S(2)}) collective-permute-start(bf16[72,4096]{1,0:T(8,128)(2,1)S(1)} %bitcast.118), channel_id=1, source_target_pairs={{0,1},{1,0},{2,3},{3,2},{4,5},{5,4},{6,7},{7,6},{8,9},{9,8},{10,11... | collective-permute-start | bytes 1769480 | tf_op jit(solution)/shard_map/cond/branch_2_fun/ppermute | solution.py:25
  73.4 28.8 %collective-permute-done.35 = bf16[144,1408]{1,0:T(8,128)(2,1)S(1)} collective-permute-done((bf16[144,1408]{1,0:T(8,128)(2,1)S(1)}, bf16[144,1408]{1,0:T(8,128)(2,1)S(1)}, u32[]{:S(2)}, u32[]{:S(2)}) %collective-permute-start.35) | collective-permute-done | bytes 405536 | tf_op jit(solution)/shard_map/cond/branch_2_fun/ppermute | solution.py:21
  102.2 0.0 collective-permute-done.34
  102.2 1.4 fusion.16
  103.6 0.6 add_rsqrt_fusion.2
  104.2 6.6 %convolution_add_fusion.2 = f32[144,1408]{1,0:T(8,128)S(1)} fusion(bf16[4096,1408]{1,0:T(8,128)(2,1)} %get-tuple-element.138, f32[4096]{0:T(1024)S(1)} %get-tuple-element.137, f32[144]{0:T(256)} %add_rsqrt_fusion.2, bf16[72,4096]{1,0:T(8,128)(2,1)} %collective-permute-done.34, bf16[72,4096]{1,0:T(8,128)(2,1)S(1)} %bitcast.120, f32[1408]{0:T(1024)S(1)} %get-tuple-element.139), kind=kOutput, calls=%fused_computation.46 | convolution fusion | flops 1665275904 | bytes 13547584 | tf_op jit(solution)/shard_map/cond/branch_2_fun/dot_general | solution.py:74
  110.8 1.0 convert_reduce_fusion.2
  112.9 8.1 %fusion.46 = f32[144,4096]{1,0:T(8,128)S(1)} fusion(bf16[144,1408]{1,0:T(8,128)(2,1)S(1)} %get-tuple-element.158, bf16[4096,1408]{1,0:T(8,128)(2,1)} %param.49), kind=kOutput, calls=%fused_computation.129 | convolution fusion | flops 1660944384 | bytes 14299136 | tf_op jit(solution)/shard_map/dot_general | solution.py:87
  121.0 0.9 slice.127
  121.9 0.0 copy-start.2
  121.9 1.5 multiply_reduce_fusion
  123.5 0.1 pad.25.clone
  123.6 2.9 %collective-permute-start.38 = (bf16[72,4096]{1,0:T(8,128)(2,1)}, bf16[72,4096]{1,0:T(8,128)(2,1)S(1)}, u32[]{:S(2)}, u32[]{:S(2)}) collective-permute-start(bf16[72,4096]{1,0:T(8,128)(2,1)} %slice.127), channel_id=1, source_target_pairs={{0,1},{1,0},{2,3},{3,2},{4,5},{5,4},{6,7},{7,6},{8,9},{9,8},{10,11... | collective-permute-start | bytes 1769480 | tf_op jit(solution)/shard_map/ppermute | solution.py:25
  126.4 0.1 maximum_maximum_fusion.1
  126.5 0.7 maximum_maximum_fusion
  127.3 5.5 %all-to-all-start.1 = ((f32[24,8,128]{2,1,0:T(8,128)}), f32[24,8,128]{2,1,0:T(8,128)S(1)}, u32[]{:S(2)}, u32[]{:S(2)}) async-start(f32[24,8,128]{2,1,0:T(8,128)} %maximum_maximum_fusion), calls=%async_computation.1 | async-start | bytes 196608 | tf_op jit(solution)/shard_map/all_to_all | solution.py:131
  132.9 0.0 copy-done.2
  132.9 0.2 fusion.38
  133.0 6.9 %all-to-all-done.1 = f32[24,8,128]{2,1,0:T(8,128)S(1)} async-done(((f32[24,8,128]{2,1,0:T(8,128)}), f32[24,8,128]{2,1,0:T(8,128)S(1)}, u32[]{:S(2)}, u32[]{:S(2)}) %all-to-all-start.1) | async-done | bytes 98336 | tf_op jit(solution)/shard_map/all_to_all | solution.py:131
  139.9 0.1 select_reduce_fusion
  140.1 0.7 broadcast_in_dim.39
  140.7 7.8 %all-to-all-start.2 = ((f32[32,8,128]{2,1,0:T(8,128)}), f32[32,8,128]{2,1,0:T(8,128)S(1)}, u32[]{:S(2)}, u32[]{:S(2)}) async-start(f32[32,8,128]{2,1,0:T(8,128)} %broadcast_in_dim.39), calls=%async_computation.2 | async-start | bytes 262144 | tf_op jit(solution)/shard_map/all_to_all | solution.py:30
  148.5 0.0 collective-permute-done.38
  148.5 0.1 slice_add_fusion
  148.6 0.0 copy-start.1
  148.6 1.0 copy-done.1
  149.7 1.9 %collective-permute-start.39 = (bf16[24,4096]{1,0:T(8,128)(2,1)S(1)}, bf16[24,4096]{1,0:T(8,128)(2,1)S(1)}, u32[]{:S(2)}, u32[]{:S(2)}) collective-permute-start(bf16[24,4096]{1,0:T(8,128)(2,1)S(1)} %get-tuple-element.185), channel_id=1, source_target_pairs={{0,2},{2,4},{4,0},{1,3},{3,5},{5,1},{6,8},{8,10},{10,6},{7,9},{9,1... | collective-permute-start | bytes 589832 | tf_op jit(solution)/shard_map/ppermute | solution.py:103
  151.6 4.3 %collective-permute-start.40 = (bf16[24,4096]{1,0:T(8,128)(2,1)S(1)}, bf16[24,4096]{1,0:T(8,128)(2,1)S(1)}, u32[]{:S(2)}, u32[]{:S(2)}) collective-permute-start(bf16[24,4096]{1,0:T(8,128)(2,1)S(1)} %get-tuple-element.186), channel_id=1, source_target_pairs={{0,4},{2,0},{4,2},{1,5},{3,1},{5,3},{6,10},{8,6},{10,8},{7,11},{9,... | collective-permute-start | bytes 589832 | tf_op jit(solution)/shard_map/ppermute | solution.py:103
  155.9 6.3 %all-to-all-done.2 = f32[32,8,128]{2,1,0:T(8,128)S(1)} async-done(((f32[32,8,128]{2,1,0:T(8,128)}), f32[32,8,128]{2,1,0:T(8,128)S(1)}, u32[]{:S(2)}, u32[]{:S(2)}) %all-to-all-start.2) | async-done | bytes 131104 | tf_op jit(solution)/shard_map/all_to_all | solution.py:30
  162.3 0.6 broadcast_in_dim.40
  162.9 5.2 %all-to-all-start.3 = ((f32[24,8,128]{2,1,0:T(8,128)}), f32[24,8,128]{2,1,0:T(8,128)S(1)}, u32[]{:S(2)}, u32[]{:S(2)}) async-start(f32[24,8,128]{2,1,0:T(8,128)} %broadcast_in_dim.40), calls=%async_computation.3 | async-start | bytes 196608 | tf_op jit(solution)/shard_map/all_to_all | solution.py:30
  168.2 0.0 collective-permute-done.39
  168.2 0.0 collective-permute-done.40
  168.2 1.3 fusion.34
  169.4 1.8 %fusion.37 = bf16[24,4096]{1,0:T(8,128)(2,1)} fusion(bf16[24,4096]{1,0:T(8,128)(2,1)S(1)} %copy-done.2, f32[24]{0:T(128)S(1)} %broadcast_multiply_fusion.4, f32[24]{0:T(128)S(1)} %add_rsqrt_fusion.4, f32[4096]{0:T(1024)S(1)} %copy-done.4, bf16[24,4096]{1,0:T(8,128)(2,1)S(1)} %collective-permute-done.40, bf16[24,4096]{1,0:T(8,128)(2,1)S(1)} %collective-permute-done.39, ...), kind=kLoop, calls=%fused_computation.98 | loop fusion | flops 1081344 | bytes 1196228 | tf_op jit(solution)/shard_map/convert_element_type | solution.py:150
  171.3 4.1 %all-to-all-done.3 = f32[24,8,128]{2,1,0:T(8,128)S(1)} async-done(((f32[24,8,128]{2,1,0:T(8,128)}), f32[24,8,128]{2,1,0:T(8,128)S(1)}, u32[]{:S(2)}, u32[]{:S(2)}) %all-to-all-start.3) | async-done | bytes 98336 | tf_op jit(solution)/shard_map/all_to_all | solution.py:30
  175.4 0.6 slice_bitcast_fusion.8
  176.0 0.5 slice.79
  176.5 0.6 slice.75
  (22 shorter events, 0.3 us)
Async XLA Ops:
  0.6 8.6 %copy-start = (s32[128,144]{0,1:T(8,128)S(1)}, s32[128,144]{0,1:T(8,128)}, u32[]{:S(2)}) copy-start(s32[128,144]{0,1:T(8,128)} %param.44) | copy-start | bytes 221188
  0.6 9.4 %copy-start.3 = (bf16[144,1408]{1,0:T(8,128)(2,1)S(1)}, bf16[144,1408]{1,0:T(8,128)(2,1)}, u32[]{:S(2)}) copy-start(bf16[144,1408]{1,0:T(8,128)(2,1)} %param.45) | copy-start | bytes 1216516
  2.5 35.1 %all-to-all-start = ((bf16[3,24,4096]{2,1,0:T(8,128)(2,1)}), bf16[3,24,4096]{2,1,0:T(8,128)(2,1)S(1)}, u32[]{:S(2)}, u32[]{:S(2)}) async-start(bf16[3,24,4096]{2,1,0:T(8,128)(2,1)} %broadcast_in_dim.31), calls=%async_computation | async-start | bytes 1179648 | tf_op jit(solution)/shard_map/all_to_all | solution.py:30
  10.1 27.5 %copy-start.4 = (f32[4096]{0:T(1024)S(1)}, f32[4096]{0:T(1024)}, u32[]{:S(2)}) copy-start(f32[4096]{0:T(1024)} %param.47) | copy-start | bytes 49156
  10.1 27.5 %copy-start.5 = (f32[1408]{0:T(1024)S(1)}, f32[1408]{0:T(1024)}, u32[]{:S(2)}) copy-start(f32[1408]{0:T(1024)} %param.48) | copy-start | bytes 16900
  10.1 27.4 %collective-permute-start.26 = (bf16[144,1408]{1,0:T(8,128)(2,1)S(1)}, bf16[144,1408]{1,0:T(8,128)(2,1)S(1)}, u32[]{:S(2)}, u32[]{:S(2)}) collective-permute-start(bf16[144,1408]{1,0:T(8,128)(2,1)S(1)} %param.27), channel_id=1, source_target_pairs={{648,0},{654,6},{660,12},{666,18},{672,24},{678,30},{684,36},{690,... | collective-permute-start | bytes 1216520 | tf_op jit(solution)/shard_map/cond/branch_27_fun/ppermute | solution.py:21
  37.6 64.6 %collective-permute-start.35 = (bf16[144,1408]{1,0:T(8,128)(2,1)S(1)}, bf16[144,1408]{1,0:T(8,128)(2,1)S(1)}, u32[]{:S(2)}, u32[]{:S(2)}) collective-permute-start(bf16[144,1408]{1,0:T(8,128)(2,1)S(1)} %get-tuple-element.141), channel_id=1, source_target_pairs={{12,0},{18,6},{24,12},{30,18},{36,24},{42,30},{48,36},{54,42},{60,... | collective-permute-start | bytes 1216520 | tf_op jit(solution)/shard_map/cond/branch_2_fun/ppermute | solution.py:21
  64.9 37.3 %collective-permute-start.34 = (bf16[72,4096]{1,0:T(8,128)(2,1)S(1)}, bf16[72,4096]{1,0:T(8,128)(2,1)}, u32[]{:S(2)}, u32[]{:S(2)}) collective-permute-start(bf16[72,4096]{1,0:T(8,128)(2,1)S(1)} %bitcast.118), channel_id=1, source_target_pairs={{0,1},{1,0},{2,3},{3,2},{4,5},{5,4},{6,7},{7,6},{8,9},{9,8},{10,11... | collective-permute-start | bytes 1769480 | tf_op jit(solution)/shard_map/cond/branch_2_fun/ppermute | solution.py:25
  121.9 11.0 %copy-start.2 = (bf16[24,4096]{1,0:T(8,128)(2,1)S(1)}, bf16[24,4096]{1,0:T(8,128)(2,1)}, u32[]{:S(2)}) copy-start(bf16[24,4096]{1,0:T(8,128)(2,1)} %param.43) | copy-start | bytes 589828
  123.6 24.9 %collective-permute-start.38 = (bf16[72,4096]{1,0:T(8,128)(2,1)}, bf16[72,4096]{1,0:T(8,128)(2,1)S(1)}, u32[]{:S(2)}, u32[]{:S(2)}) collective-permute-start(bf16[72,4096]{1,0:T(8,128)(2,1)} %slice.127), channel_id=1, source_target_pairs={{0,1},{1,0},{2,3},{3,2},{4,5},{5,4},{6,7},{7,6},{8,9},{9,8},{10,11... | collective-permute-start | bytes 1769480 | tf_op jit(solution)/shard_map/ppermute | solution.py:25
  127.3 12.7 %all-to-all-start.1 = ((f32[24,8,128]{2,1,0:T(8,128)}), f32[24,8,128]{2,1,0:T(8,128)S(1)}, u32[]{:S(2)}, u32[]{:S(2)}) async-start(f32[24,8,128]{2,1,0:T(8,128)} %maximum_maximum_fusion), calls=%async_computation.1 | async-start | bytes 196608 | tf_op jit(solution)/shard_map/all_to_all | solution.py:131
  140.7 21.5 %all-to-all-start.2 = ((f32[32,8,128]{2,1,0:T(8,128)}), f32[32,8,128]{2,1,0:T(8,128)S(1)}, u32[]{:S(2)}, u32[]{:S(2)}) async-start(f32[32,8,128]{2,1,0:T(8,128)} %broadcast_in_dim.39), calls=%async_computation.2 | async-start | bytes 262144 | tf_op jit(solution)/shard_map/all_to_all | solution.py:30
  148.6 1.0 copy-start.1
  149.7 18.5 %collective-permute-start.39 = (bf16[24,4096]{1,0:T(8,128)(2,1)S(1)}, bf16[24,4096]{1,0:T(8,128)(2,1)S(1)}, u32[]{:S(2)}, u32[]{:S(2)}) collective-permute-start(bf16[24,4096]{1,0:T(8,128)(2,1)S(1)} %get-tuple-element.185), channel_id=1, source_target_pairs={{0,2},{2,4},{4,0},{1,3},{3,5},{5,1},{6,8},{8,10},{10,6},{7,9},{9,1... | collective-permute-start | bytes 589832 | tf_op jit(solution)/shard_map/ppermute | solution.py:103
  151.6 16.5 %collective-permute-start.40 = (bf16[24,4096]{1,0:T(8,128)(2,1)S(1)}, bf16[24,4096]{1,0:T(8,128)(2,1)S(1)}, u32[]{:S(2)}, u32[]{:S(2)}) collective-permute-start(bf16[24,4096]{1,0:T(8,128)(2,1)S(1)} %get-tuple-element.186), channel_id=1, source_target_pairs={{0,4},{2,0},{4,2},{1,5},{3,1},{5,3},{6,10},{8,6},{10,8},{7,11},{9,... | collective-permute-start | bytes 589832 | tf_op jit(solution)/shard_map/ppermute | solution.py:103
  162.9 12.5 %all-to-all-start.3 = ((f32[24,8,128]{2,1,0:T(8,128)}), f32[24,8,128]{2,1,0:T(8,128)S(1)}, u32[]{:S(2)}, u32[]{:S(2)}) async-start(f32[24,8,128]{2,1,0:T(8,128)} %broadcast_in_dim.40), calls=%async_computation.3 | async-start | bytes 196608 | tf_op jit(solution)/shard_map/all_to_all | solution.py:30

commit v3 on v2

--- a/solution.py
+++ b/solution.py
@@ -77,21 +77,21 @@
             loss_part = jnp.sum(weight * error * error) / (2.0 * tokens * features)
             grad_out = (weight * error).astype(jnp.bfloat16)
             bias_part = jnp.sum(grad_out.astype(jnp.float32), axis=0) / tokens
-            return lax.optimization_barrier((grad_out, loss_part, bias_part, other, inverse))
+            grad_all = lax.dot_general(
+                grad_out, projection, (((1,), (1,)), ((), ())), preferred_element_type=jnp.float32
+            )
+            return lax.optimization_barrier((grad_all, loss_part, bias_part, other, inverse))
 
         return branch
 
-    grad_out, loss_part, bias_part, other, block_inverse = lax.switch(
+    grad_all, loss_part, bias_part, other, block_inverse = lax.switch(
         turn % N_ZH, [near(s) for s in range(N_ZH)], moved, gathered, weight
     )
-    grad_all = lax.dot_general(
-        grad_out, projection, (((1,), (1,)), ((), ())), preferred_element_type=jnp.float32
-    )
-    grad_all = lax.optimization_barrier(grad_all)
     block = jnp.concatenate([gathered.reshape(-1, width), other], 0)
     gain_part = jnp.sum(grad_all * (block.astype(jnp.float32) * block_inverse), axis=0) / tokens
     half = block_rows // N_C
-    own_rows, far_rows = grad_all[:half], grad_all[half:].astype(jnp.bfloat16)
+    own_rows = grad_all[:half]
+    far_rows = grad_all[half:].astype(jnp.bfloat16)
     summed = own_rows + swap_cores(far_rows).astype(jnp.float32)
     summed = summed.reshape(N_ZL, portion_rows, width)
     at = lax.axis_index("zl")
@@ -132,7 +132,8 @@
     line = lax.broadcasted_iota(jnp.int32, lines.shape, 1)
     sender = lax.broadcasted_iota(jnp.int32, lines.shape, 0) % n_tensor
     lines = jnp.sum(jnp.where((line < gain_each) | (sender == column), lines, 0.0), axis=0)
-    lines = jnp.sum(spread(lines, ("y", "zh"), N_Y * N_ZH), axis=0)
+    lines = jnp.sum(spread(lines, "y", N_Y), axis=0)
+    lines = jnp.sum(spread(lines, "zh", N_ZH), axis=0)
     lines = spread(lines, group, peers)
     shared = lines[:, :gain_each].reshape(peers * gain_each, LANES)
     gain_gradient_mean = shared[:gain_lines].reshape(width)

time: 178 us -> 185 us (1.039)
  waiting for transfers between devices: 66.7 us -> 76.2 us
  matrix products: 14.7 us -> 10.3 us
  starting transfers between devices: 76 us -> 79.1 us
    ppermute x2, waiting for transfers between devices: 0.01 us -> 5.83 us  [shards(): pieces.append(lax.ppermute(piece.astype(jnp.bfloat16), 'zl', ring))]
    all_to_all x3 -> x4, waiting for transfers between devices: 10.4 us -> 15.7 us  [spread(): return lax.all_to_all(copies, axes, 0, 0, tiled=True)]
    dot_general x1, matrix products: 8.12 us -> 3.84 us  [branch(): lax.dot_general(grad_out, projection, (((1,), (1,)), ((), ())), preferred...]
    all_to_all x3 -> x4, starting transfers between devices: 19 us -> 22.3 us  [spread(): return lax.all_to_all(copies, axes, 0, 0, tiled=True)]
    all_to_all x1, waiting for transfers between devices: 6.86 us -> 4.9 us  [shards(): lines = lax.all_to_all(lines, group, 0, 0, tiled=True)]
    broadcast_in_dim x3 -> x4, local copies, waits for them, and re-layouts: 3.16 us -> 3.74 us  [spread(): jnp.broadcast_to(value[None], (count, *value.shape))]
  transfers between devices with their start and end apart: 10 -> 11, of which waited for: 5 -> 7; matrix products, arithmetic and copies ran while one was open for 4% -> 3% of each run, Pallas kernels for 0% -> 0%
where the time goes in v3:
time: 185 us
  starting transfers between devices  79.1 us (43%)
  waiting for transfers between devices  76.2 us (41%)
  matrix products  10.3 us (6%)
  other arithmetic  8.66 us (5%)
  local copies, waits for them, and re-layouts  7.52 us (4%)
    ppermute x2, waiting for transfers between devices, pull(): lax.ppermute(value, DP, [((i + steps) % N_DP, i) for i in range(N_DP)])  49.7 us
    ppermute x2, starting transfers between devices, pull(): lax.ppermute(value, DP, [((i + steps) % N_DP, i) for i in range(N_DP)])  33.9 us
    all_to_all x4, starting transfers between devices, spread(): return lax.all_to_all(copies, axes, 0, 0, tiled=True)  22.3 us
    all_to_all x4, waiting for transfers between devices, spread(): return lax.all_to_all(copies, axes, 0, 0, tiled=True)  15.7 us
    ppermute x2, starting transfers between devices, swap_cores(): return lax.ppermute(value, 'c', [(0, 1), (1, 0)])  10.3 us
    dot_general x1, matrix products, branch(): jnp.dot(rows, projection, preferred_element_type=jnp.float32) + bias  6.5 us
    all_to_all x1, starting transfers between devices, shards(): lines = lax.all_to_all(lines, group, 0, 0, tiled=True)  6.37 us
    ppermute x2, starting transfers between devices, shards(): pieces.append(lax.ppermute(piece.astype(jnp.bfloat16), 'zl', ring))  6.18 us
  transfers between devices with their start and end apart: 11, of which 7 were waited for; matrix products, arithmetic and copies ran while one was open for 3% of the time, Pallas kernels for 0%

profile of v3, /device:TPU:1, one launch (start us, length us, event | category | flops | bytes accessed | tf_op | source)
XLA Modules:
  0.0 184.6 jit_solution(8413362824181236606)
XLA Ops:
  0.6 0.0 copy-start
  0.6 0.0 copy-start.7
  0.7 1.9 %broadcast_in_dim.33 = bf16[3,24,4096]{2,1,0:T(8,128)(2,1)} broadcast(bf16[24,4096]{1,0:T(8,128)(2,1)} %param.43), dimensions={1,2} | broadcast | bytes 786432 | tf_op jit(solution)/shard_map/broadcast_in_dim | solution.py:29
  2.5 6.0 %all-to-all-start = ((bf16[3,24,4096]{2,1,0:T(8,128)(2,1)}), bf16[3,24,4096]{2,1,0:T(8,128)(2,1)S(1)}, u32[]{:S(2)}, u32[]{:S(2)}) async-start(bf16[3,24,4096]{2,1,0:T(8,128)(2,1)} %broadcast_in_dim.33), calls=%async_computation | async-start | bytes 1179648 | tf_op jit(solution)/shard_map/all_to_all | solution.py:30
  9.2 0.2 dynamic-slice_reduce_fusion
  9.4 0.2 convert_reduce_fusion.4
  9.6 0.1 div.77
  9.7 0.1 select_n.154
  9.8 0.1 select_n.156
  9.9 0.1 pad.26.clone
  10.0 0.1 pad.23.clone
  10.1 27.4 %conditional.2 = (bf16[144,1408]{1,0:T(8,128)(2,1)S(1)}) conditional(s32[]{:T(128)} %clamp.7, bf16[144,1408]{1,0:T(8,128)(2,1)S(1)} %copy-done.7, bf16[144,1408]{1,0:T(8,128)(2,1)S(1)} %copy-done.7, bf16[144,1408]{1,0:T(8,128)(2,1)S(1)} %copy-done.7, bf16[144,1408]{1,0:T(8,128)(2,1)S(1)} %copy-done.7, ...), branch_computations={%region_1.2_spmd, %region_2.3_spmd, %region_3.4_spmd, %region_4.5_... | conditional | bytes 2433072 | solution.py:60
  10.1 6.7 %collective-permute-start.26 = (bf16[144,1408]{1,0:T(8,128)(2,1)S(1)}, bf16[144,1408]{1,0:T(8,128)(2,1)S(1)}, u32[]{:S(2)}, u32[]{:S(2)}) collective-permute-start(bf16[144,1408]{1,0:T(8,128)(2,1)S(1)} %param.27), channel_id=1, source_target_pairs={{648,0},{654,6},{660,12},{666,18},{672,24},{678,30},{684,36},{690,... | collective-permute-start | bytes 1216520 | tf_op jit(solution)/shard_map/cond/branch_27_fun/ppermute | solution.py:21
  16.8 20.7 %collective-permute-done.26 = bf16[144,1408]{1,0:T(8,128)(2,1)S(1)} collective-permute-done((bf16[144,1408]{1,0:T(8,128)(2,1)S(1)}, bf16[144,1408]{1,0:T(8,128)(2,1)S(1)}, u32[]{:S(2)}, u32[]{:S(2)}) %collective-permute-start.26) | collective-permute-done | bytes 405536 | tf_op jit(solution)/shard_map/cond/branch_27_fun/ppermute | solution.py:21
  37.5 0.1 pad_maximum_fusion.12
  37.6 0.0 all-to-all-done
  37.6 0.0 copy-done.13
  37.6 77.4 %conditional.3 = (f32[144,4096]{1,0:T(8,128)S(1)}, f32[]{:T(128)}, f32[1408]{0:T(1024)S(1)}, bf16[72,4096]{1,0:T(8,128)(2,1)}, f32[144,1]{0,1:T(1,128)}) conditional(s32[]{:T(128)} %clamp.6, (f32[144,1]{0,1:T(1,128)S(1)}, bf16[3,24,4096]{2,1,0:T(8,128)(2,1)S(1)}, f32[4096]{0:T(1024)S(1)}, ...), branch_computations={%region_34.0_spmd, %region_38.42_spmd, %region_42.46_spmd, %region... | conditional | flops 3332192256 | bytes 72424784 | solution.py:87
  37.9 27.3 %collective-permute-start.35 = (bf16[144,1408]{1,0:T(8,128)(2,1)S(1)}, bf16[144,1408]{1,0:T(8,128)(2,1)S(1)}, u32[]{:S(2)}, u32[]{:S(2)}) collective-permute-start(bf16[144,1408]{1,0:T(8,128)(2,1)S(1)} %get-tuple-element.141), channel_id=1, source_target_pairs={{12,0},{18,6},{24,12},{30,18},{36,24},{42,30},{48,36},{54,42},{60,... | collective-permute-start | bytes 1216520 | tf_op jit(solution)/shard_map/cond/branch_2_fun/ppermute | solution.py:21
  65.2 8.2 %collective-permute-start.34 = (bf16[72,4096]{1,0:T(8,128)(2,1)S(1)}, bf16[72,4096]{1,0:T(8,128)(2,1)S(1)}, u32[]{:S(2)}, u32[]{:S(2)}) collective-permute-start(bf16[72,4096]{1,0:T(8,128)(2,1)S(1)} %bitcast.132), channel_id=1, source_target_pairs={{0,1},{1,0},{2,3},{3,2},{4,5},{5,4},{6,7},{7,6},{8,9},{9,8},{10,11... | collective-permute-start | bytes 1769480 | tf_op jit(solution)/shard_map/cond/branch_2_fun/ppermute | solution.py:25
  73.4 29.0 %collective-permute-done.35 = bf16[144,1408]{1,0:T(8,128)(2,1)S(1)} collective-permute-done((bf16[144,1408]{1,0:T(8,128)(2,1)S(1)}, bf16[144,1408]{1,0:T(8,128)(2,1)S(1)}, u32[]{:S(2)}, u32[]{:S(2)}) %collective-permute-start.35) | collective-permute-done | bytes 405536 | tf_op jit(solution)/shard_map/cond/branch_2_fun/ppermute | solution.py:21
  102.5 0.0 collective-permute-done.34
  102.5 0.3 fusion.16
  102.9 0.0 slice-start.6
  102.9 0.0 slice-start.7
  102.9 0.0 slice-start.8
  102.9 6.5 %convolution_add_fusion.2 = f32[144,1408]{1,0:T(8,128)S(1)} fusion(bf16[4096,1408]{1,0:T(8,128)(2,1)} %get-tuple-element.138, f32[4096]{0:T(1024)S(1)} %get-tuple-element.137, f32[144]{0:T(256)S(1)} %add_rsqrt_fusion.2, bf16[72,4096]{1,0:T(8,128)(2,1)S(1)} %collective-permute-done.34, bf16[72,4096]{1,0:T(8,128)(2,1)S(1)} %bitcast.134, ...), kind=kOutput, calls=%fused_computation.46 | convolution fusion | flops 1665275904 | bytes 13547584 | tf_op jit(solution)/shard_map/cond/branch_2_fun/dot_general | solution.py:74
  109.4 1.0 convert_reduce_fusion.2
  110.4 0.0 slice-done.7
  110.4 0.1 slice-done.8
  110.5 3.8 %fusion.48 = f32[144,4096]{1,0:T(8,128)S(1)} fusion(bf16[144,1408]{1,0:T(8,128)(2,1)S(1)} %get-tuple-element.170, bf16[4096,1408]{1,0:T(8,128)(2,1)S(1)} %bitcast.122), kind=kOutput, calls=%fused_computation.131 | convolution fusion | flops 1660944384 | bytes 14299136 | tf_op jit(solution)/shard_map/cond/branch_2_fun/dot_general | solution.py:80
  115.0 0.0 copy-start.6
  115.0 1.5 multiply_reduce_fusion
  116.6 0.1 pad.25.clone
  116.7 0.1 maximum_maximum_fusion.1
  116.8 0.7 maximum_maximum_fusion
  117.5 6.4 %all-to-all-start.1 = ((f32[24,8,128]{2,1,0:T(8,128)}), f32[24,8,128]{2,1,0:T(8,128)S(1)}, u32[]{:S(2)}, u32[]{:S(2)}) async-start(f32[24,8,128]{2,1,0:T(8,128)} %maximum_maximum_fusion), calls=%async_computation.1 | async-start | bytes 196608 | tf_op jit(solution)/shard_map/all_to_all | solution.py:131
  123.9 0.1 slice.126
  124.0 2.1 %collective-permute-start.38 = (bf16[72,4096]{1,0:T(8,128)(2,1)S(1)}, bf16[72,4096]{1,0:T(8,128)(2,1)}, u32[]{:S(2)}, u32[]{:S(2)}) collective-permute-start(bf16[72,4096]{1,0:T(8,128)(2,1)S(1)} %slice.126), channel_id=1, source_target_pairs={{0,1},{1,0},{2,3},{3,2},{4,5},{5,4},{6,7},{7,6},{8,9},{9,8},{10,11... | collective-permute-start | bytes 1769480 | tf_op jit(solution)/shard_map/ppermute | solution.py:25
  126.1 4.9 %all-to-all-done.1 = f32[24,8,128]{2,1,0:T(8,128)S(1)} async-done(((f32[24,8,128]{2,1,0:T(8,128)}), f32[24,8,128]{2,1,0:T(8,128)S(1)}, u32[]{:S(2)}, u32[]{:S(2)}) %all-to-all-start.1) | async-done | bytes 98336 | tf_op jit(solution)/shard_map/all_to_all | solution.py:131
  131.0 0.1 select_reduce_fusion
  131.2 0.6 broadcast_in_dim.41
  131.8 6.6 %all-to-all-start.2 = ((f32[8,8,128]{2,1,0:T(8,128)}), f32[8,8,128]{2,1,0:T(8,128)S(1)}, u32[]{:S(2)}, u32[]{:S(2)}) async-start(f32[8,8,128]{2,1,0:T(8,128)} %broadcast_in_dim.41), calls=%async_computation.2 | async-start | bytes 65536 | tf_op jit(solution)/shard_map/all_to_all | solution.py:30
  138.4 0.0 copy-done.6
  138.4 0.2 fusion.38
  138.6 6.8 %all-to-all-done.2 = f32[8,8,128]{2,1,0:T(8,128)S(1)} async-done(((f32[8,8,128]{2,1,0:T(8,128)}), f32[8,8,128]{2,1,0:T(8,128)S(1)}, u32[]{:S(2)}, u32[]{:S(2)}) %all-to-all-start.2) | async-done | bytes 32800 | tf_op jit(solution)/shard_map/all_to_all | solution.py:30
  145.4 0.6 broadcast_in_dim.42
  146.0 3.3 %all-to-all-start.3 = ((f32[4,8,128]{2,1,0:T(8,128)}), f32[4,8,128]{2,1,0:T(8,128)S(1)}, u32[]{:S(2)}, u32[]{:S(2)}) async-start(f32[4,8,128]{2,1,0:T(8,128)} %broadcast_in_dim.42), calls=%async_computation.3 | async-start | bytes 32768 | tf_op jit(solution)/shard_map/all_to_all | solution.py:30
  149.3 8.9 %all-to-all-done.3 = f32[4,8,128]{2,1,0:T(8,128)S(1)} async-done(((f32[4,8,128]{2,1,0:T(8,128)}), f32[4,8,128]{2,1,0:T(8,128)S(1)}, u32[]{:S(2)}, u32[]{:S(2)}) %all-to-all-start.3) | async-done | bytes 16416 | tf_op jit(solution)/shard_map/all_to_all | solution.py:30
  158.3 0.7 broadcast_in_dim.43
  158.9 6.4 %all-to-all-start.4 = ((f32[24,8,128]{2,1,0:T(8,128)}), f32[24,8,128]{2,1,0:T(8,128)S(1)}, u32[]{:S(2)}, u32[]{:S(2)}) async-start(f32[24,8,128]{2,1,0:T(8,128)} %broadcast_in_dim.43), calls=%async_computation.4 | async-start | bytes 196608 | tf_op jit(solution)/shard_map/all_to_all | solution.py:30
  165.3 0.0 collective-permute-done.38
  165.3 1.2 convert_add_fusion
  166.6 1.0 copy-done.5
  167.6 3.3 %collective-permute-start.39 = (bf16[24,4096]{1,0:T(8,128)(2,1)S(1)}, bf16[24,4096]{1,0:T(8,128)(2,1)S(1)}, u32[]{:S(2)}, u32[]{:S(2)}) collective-permute-start(bf16[24,4096]{1,0:T(8,128)(2,1)S(1)} %get-tuple-element.185), channel_id=1, source_target_pairs={{0,2},{2,4},{4,0},{1,3},{3,5},{5,1},{6,8},{8,10},{10,6},{7,9},{9,1... | collective-permute-start | bytes 589832 | tf_op jit(solution)/shard_map/ppermute | solution.py:103
  170.9 2.9 %collective-permute-start.40 = (bf16[24,4096]{1,0:T(8,128)(2,1)S(1)}, bf16[24,4096]{1,0:T(8,128)(2,1)S(1)}, u32[]{:S(2)}, u32[]{:S(2)}) collective-permute-start(bf16[24,4096]{1,0:T(8,128)(2,1)S(1)} %get-tuple-element.186), channel_id=1, source_target_pairs={{0,4},{2,0},{4,2},{1,5},{3,1},{5,3},{6,10},{8,6},{10,8},{7,11},{9,... | collective-permute-start | bytes 589832 | tf_op jit(solution)/shard_map/ppermute | solution.py:103
  173.8 0.0 all-to-all-done.4
  173.9 0.5 slice.78
  174.4 0.6 slice.74
  175.0 0.6 slice_bitcast_fusion.8
  175.6 1.0 collective-permute-done.39
  176.6 4.9 %collective-permute-done.40 = bf16[24,4096]{1,0:T(8,128)(2,1)S(1)} collective-permute-done((bf16[24,4096]{1,0:T(8,128)(2,1)S(1)}, bf16[24,4096]{1,0:T(8,128)(2,1)S(1)}, u32[]{:S(2)}, u32[]{:S(2)}) %collective-permute-start.40) | collective-permute-done | bytes 196640 | tf_op jit(solution)/shard_map/ppermute | solution.py:103
  181.5 1.3 fusion.34
  182.7 1.8 fusion.37
  (36 shorter events, 0.3 us)
Async XLA Ops:
  0.6 8.6 %copy-start = (s32[128,144]{0,1:T(8,128)S(1)}, s32[128,144]{0,1:T(8,128)}, u32[]{:S(2)}) copy-start(s32[128,144]{0,1:T(8,128)} %param.44) | copy-start | bytes 221188
  0.6 9.4 %copy-start.7 = (bf16[144,1408]{1,0:T(8,128)(2,1)S(1)}, bf16[144,1408]{1,0:T(8,128)(2,1)}, u32[]{:S(2)}) copy-start(bf16[144,1408]{1,0:T(8,128)(2,1)} %param.45) | copy-start | bytes 1216516
  2.5 35.1 %all-to-all-start = ((bf16[3,24,4096]{2,1,0:T(8,128)(2,1)}), bf16[3,24,4096]{2,1,0:T(8,128)(2,1)S(1)}, u32[]{:S(2)}, u32[]{:S(2)}) async-start(bf16[3,24,4096]{2,1,0:T(8,128)(2,1)} %broadcast_in_dim.33), calls=%async_computation | async-start | bytes 1179648 | tf_op jit(solution)/shard_map/all_to_all | solution.py:30
  10.1 27.5 %copy-start.8 = (f32[4096]{0:T(1024)S(1)}, f32[4096]{0:T(1024)}, u32[]{:S(2)}) copy-start(f32[4096]{0:T(1024)} %param.47) | copy-start | bytes 49156
  10.1 27.5 %copy-start.13 = (f32[1408]{0:T(1024)S(1)}, f32[1408]{0:T(1024)}, u32[]{:S(2)}) copy-start(f32[1408]{0:T(1024)} %param.48) | copy-start | bytes 16900
  10.1 27.4 %collective-permute-start.26 = (bf16[144,1408]{1,0:T(8,128)(2,1)S(1)}, bf16[144,1408]{1,0:T(8,128)(2,1)S(1)}, u32[]{:S(2)}, u32[]{:S(2)}) collective-permute-start(bf16[144,1408]{1,0:T(8,128)(2,1)S(1)} %param.27), channel_id=1, source_target_pairs={{648,0},{654,6},{660,12},{666,18},{672,24},{678,30},{684,36},{690,... | collective-permute-start | bytes 1216520 | tf_op jit(solution)/shard_map/cond/branch_27_fun/ppermute | solution.py:21
  37.9 64.6 %collective-permute-start.35 = (bf16[144,1408]{1,0:T(8,128)(2,1)S(1)}, bf16[144,1408]{1,0:T(8,128)(2,1)S(1)}, u32[]{:S(2)}, u32[]{:S(2)}) collective-permute-start(bf16[144,1408]{1,0:T(8,128)(2,1)S(1)} %get-tuple-element.141), channel_id=1, source_target_pairs={{12,0},{18,6},{24,12},{30,18},{36,24},{42,30},{48,36},{54,42},{60,... | collective-permute-start | bytes 1216520 | tf_op jit(solution)/shard_map/cond/branch_2_fun/ppermute | solution.py:21
  65.2 37.3 %collective-permute-start.34 = (bf16[72,4096]{1,0:T(8,128)(2,1)S(1)}, bf16[72,4096]{1,0:T(8,128)(2,1)S(1)}, u32[]{:S(2)}, u32[]{:S(2)}) collective-permute-start(bf16[72,4096]{1,0:T(8,128)(2,1)S(1)} %bitcast.132), channel_id=1, source_target_pairs={{0,1},{1,0},{2,3},{3,2},{4,5},{5,4},{6,7},{7,6},{8,9},{9,8},{10,11... | collective-permute-start | bytes 1769480 | tf_op jit(solution)/shard_map/cond/branch_2_fun/ppermute | solution.py:25
  102.5 6.9 %copy-start.3 = (bf16[72,4096]{1,0:T(8,128)(2,1)}, bf16[72,4096]{1,0:T(8,128)(2,1)S(1)}, u32[]{:S(2)}) copy-start(bf16[72,4096]{1,0:T(8,128)(2,1)S(1)} %collective-permute-done.34) | copy-start | bytes 1769476 | tf_op jit(solution)/shard_map/cond
  102.8 6.6 %copy-start.11 = (f32[144]{0:T(256)}, f32[144]{0:T(256)S(1)}, u32[]{:S(2)}) copy-start(f32[144]{0:T(256)S(1)} %add_rsqrt_fusion.2) | copy-start | bytes 1732 | tf_op jit(solution)/shard_map/cond
  102.9 7.6 %slice-start.6 = ((s8[11534336]{0:T(1024)(128)(4,1)}), s8[4194304]{0:T(1024)(128)(4,1)S(1)}, s32[]{:S(2)}) async-start(s8[11534336]{0:T(1024)(128)(4,1)} %bitcast.121), calls=%async_computation.11 | async-start | bytes 8388608 | tf_op jit(solution)/shard_map/cond
  102.9 7.5 %slice-start.7 = ((s8[11534336]{0:T(1024)(128)(4,1)}), s8[4194304]{0:T(1024)(128)(4,1)S(1)}, s32[]{:S(2)}) async-start(s8[11534336]{0:T(1024)(128)(4,1)} %bitcast.121), calls=%async_computation.12 | async-start | bytes 8388608 | tf_op jit(solution)/shard_map/cond
  102.9 7.6 %slice-start.8 = ((s8[11534336]{0:T(1024)(128)(4,1)}), s8[3145728]{0:T(1024)(128)(4,1)S(1)}, s32[]{:S(2)}) async-start(s8[11534336]{0:T(1024)(128)(4,1)} %bitcast.121), calls=%async_computation.13 | async-start | bytes 6291456 | tf_op jit(solution)/shard_map/cond
  115.0 23.4 %copy-start.6 = (bf16[24,4096]{1,0:T(8,128)(2,1)S(1)}, bf16[24,4096]{1,0:T(8,128)(2,1)}, u32[]{:S(2)}) copy-start(bf16[24,4096]{1,0:T(8,128)(2,1)} %param.43) | copy-start | bytes 589828
  117.5 13.5 %all-to-all-start.1 = ((f32[24,8,128]{2,1,0:T(8,128)}), f32[24,8,128]{2,1,0:T(8,128)S(1)}, u32[]{:S(2)}, u32[]{:S(2)}) async-start(f32[24,8,128]{2,1,0:T(8,128)} %maximum_maximum_fusion), calls=%async_computation.1 | async-start | bytes 196608 | tf_op jit(solution)/shard_map/all_to_all | solution.py:131
  124.0 41.4 %collective-permute-start.38 = (bf16[72,4096]{1,0:T(8,128)(2,1)S(1)}, bf16[72,4096]{1,0:T(8,128)(2,1)}, u32[]{:S(2)}, u32[]{:S(2)}) collective-permute-start(bf16[72,4096]{1,0:T(8,128)(2,1)S(1)} %slice.126), channel_id=1, source_target_pairs={{0,1},{1,0},{2,3},{3,2},{4,5},{5,4},{6,7},{7,6},{8,9},{9,8},{10,11... | collective-permute-start | bytes 1769480 | tf_op jit(solution)/shard_map/ppermute | solution.py:25
  131.8 13.6 %all-to-all-start.2 = ((f32[8,8,128]{2,1,0:T(8,128)}), f32[8,8,128]{2,1,0:T(8,128)S(1)}, u32[]{:S(2)}, u32[]{:S(2)}) async-start(f32[8,8,128]{2,1,0:T(8,128)} %broadcast_in_dim.41), calls=%async_computation.2 | async-start | bytes 65536 | tf_op jit(solution)/shard_map/all_to_all | solution.py:30
  146.0 12.2 %all-to-all-start.3 = ((f32[4,8,128]{2,1,0:T(8,128)}), f32[4,8,128]{2,1,0:T(8,128)S(1)}, u32[]{:S(2)}, u32[]{:S(2)}) async-start(f32[4,8,128]{2,1,0:T(8,128)} %broadcast_in_dim.42), calls=%async_computation.3 | async-start | bytes 32768 | tf_op jit(solution)/shard_map/all_to_all | solution.py:30
  158.9 14.9 %all-to-all-start.4 = ((f32[24,8,128]{2,1,0:T(8,128)}), f32[24,8,128]{2,1,0:T(8,128)S(1)}, u32[]{:S(2)}, u32[]{:S(2)}) async-start(f32[24,8,128]{2,1,0:T(8,128)} %broadcast_in_dim.43), calls=%async_computation.4 | async-start | bytes 196608 | tf_op jit(solution)/shard_map/all_to_all | solution.py:30
  166.5 1.0 copy-start.5
  167.6 9.0 %collective-permute-start.39 = (bf16[24,4096]{1,0:T(8,128)(2,1)S(1)}, bf16[24,4096]{1,0:T(8,128)(2,1)S(1)}, u32[]{:S(2)}, u32[]{:S(2)}) collective-permute-start(bf16[24,4096]{1,0:T(8,128)(2,1)S(1)} %get-tuple-element.185), channel_id=1, source_target_pairs={{0,2},{2,4},{4,0},{1,3},{3,5},{5,1},{6,8},{8,10},{10,6},{7,9},{9,1... | collective-permute-start | bytes 589832 | tf_op jit(solution)/shard_map/ppermute | solution.py:103
  170.9 10.5 %collective-permute-start.40 = (bf16[24,4096]{1,0:T(8,128)(2,1)S(1)}, bf16[24,4096]{1,0:T(8,128)(2,1)S(1)}, u32[]{:S(2)}, u32[]{:S(2)}) collective-permute-start(bf16[24,4096]{1,0:T(8,128)(2,1)S(1)} %get-tuple-element.186), channel_id=1, source_target_pairs={{0,4},{2,0},{4,2},{1,5},{3,1},{5,3},{6,10},{8,6},{10,8},{7,11},{9,... | collective-permute-start | bytes 589832 | tf_op jit(solution)/shard_map/ppermute | solution.py:103

commit v4 on v3

--- a/solution.py
+++ b/solution.py
@@ -103,9 +103,9 @@
         pieces.append(lax.ppermute(piece.astype(jnp.bfloat16), "zl", ring))
 
     n_tensor = N_ZL * N_C
-    peers = N_X * n_tensor
+    peers = N_ZH * n_tensor
     gain_lines, bias_lines = width // LANES, columns // LANES
-    gain_each, bias_each = -(-(gain_lines + 1) // peers), -(-bias_lines // N_X)
+    gain_each, bias_each = -(-(gain_lines + 1) // peers), -(-bias_lines // N_ZH)
     used = gain_each + bias_each
     each = -(-used // 8) * 8
     shared = jnp.concatenate(
@@ -116,32 +116,31 @@
         ],
         0,
     ).reshape(peers, gain_each, LANES)
-    by_x = jnp.pad(bias_part.reshape(bias_lines, LANES), ((0, N_X * bias_each - bias_lines), (0, 0)))
-    by_x = jnp.broadcast_to(by_x.reshape(N_X, 1, bias_each, LANES), (N_X, n_tensor, bias_each, LANES))
+    by_zh = jnp.pad(bias_part.reshape(bias_lines, LANES), ((0, N_ZH * bias_each - bias_lines), (0, 0)))
+    by_zh = jnp.broadcast_to(by_zh.reshape(N_ZH, 1, bias_each, LANES), (N_ZH, n_tensor, bias_each, LANES))
     lines = jnp.concatenate(
         [
             shared,
-            by_x.reshape(peers, bias_each, LANES),
+            by_zh.reshape(peers, bias_each, LANES),
             jnp.zeros((peers, each - used, LANES), jnp.float32),
         ],
         1,
     )
-    group = ("x", *TENSOR)
+    group = ("zh", *TENSOR)
     column = lax.axis_index("zl") * N_C + core
     lines = lax.all_to_all(lines, group, 0, 0, tiled=True)
     line = lax.broadcasted_iota(jnp.int32, lines.shape, 1)
     sender = lax.broadcasted_iota(jnp.int32, lines.shape, 0) % n_tensor
     lines = jnp.sum(jnp.where((line < gain_each) | (sender == column), lines, 0.0), axis=0)
-    lines = jnp.sum(spread(lines, "y", N_Y), axis=0)
-    lines = jnp.sum(spread(lines, "zh", N_ZH), axis=0)
+    lines = jnp.sum(spread(lines, ("x", "y"), N_X * N_Y), axis=0)
     lines = spread(lines, group, peers)
     shared = lines[:, :gain_each].reshape(peers * gain_each, LANES)
     gain_gradient_mean = shared[:gain_lines].reshape(width)
     distill_loss = shared[gain_lines, 0]
-    by_x = lax.dynamic_slice_in_dim(
-        lines[:, gain_each:used].reshape(N_X, n_tensor, bias_each, LANES), column, 1, 1
+    by_zh = lax.dynamic_slice_in_dim(
+        lines[:, gain_each:used].reshape(N_ZH, n_tensor, bias_each, LANES), column, 1, 1
     )
-    grad_bias = by_x.reshape(N_X * bias_each, LANES)[:bias_lines].reshape(columns)
+    grad_bias = by_zh.reshape(N_ZH * bias_each, LANES)[:bias_lines].reshape(columns)
 
     unscaled, inverse = normalized(hidden)
     for piece in pieces:

time: 185 us -> 175 us (0.946)
  waiting for transfers between devices: 76.2 us -> 70 us
  starting transfers between devices: 79.1 us -> 76.1 us
    all_to_all x4 -> x3, waiting for transfers between devices: 15.7 us -> 9.63 us  [spread(): return lax.all_to_all(copies, axes, 0, 0, tiled=True)]
    ppermute x2, waiting for transfers between devices: 5.83 us -> 0.01 us  [shards(): pieces.append(lax.ppermute(piece.astype(jnp.bfloat16), 'zl', ring))]
    all_to_all x1, waiting for transfers between devices: 4.9 us -> 10.6 us  [shards(): lines = lax.all_to_all(lines, group, 0, 0, tiled=True)]
    all_to_all x1, starting transfers between devices: 6.37 us -> 3.67 us  [shards(): lines = lax.all_to_all(lines, group, 0, 0, tiled=True)]
    all_to_all x4 -> x3, starting transfers between devices: 22.3 us -> 21.2 us  [spread(): return lax.all_to_all(copies, axes, 0, 0, tiled=True)]
    broadcast_in_dim x4 -> x3, local copies, waits for them, and re-layouts: 3.74 us -> 3.15 us  [spread(): jnp.broadcast_to(value[None], (count, *value.shape))]
  transfers between devices with their start and end apart: 11 -> 10, of which waited for: 7 -> 5; matrix products, arithmetic and copies ran while one was open for 3% -> 4% of each run, Pallas kernels for 0% -> 0%
where the time goes in v4:
time: 175 us; the launch traced here: 174 us
  starting transfers between devices  76.1 us (43%)
  waiting for transfers between devices  70 us (40%)
  matrix products  10.3 us (6%)
  local copies, waits for them, and re-layouts  7.73 us (4%)
  other arithmetic  7.59 us (4%)
    ppermute x2, waiting for transfers between devices, pull(): lax.ppermute(value, DP, [((i + steps) % N_DP, i) for i in range(N_DP)])  49.7 us
    ppermute x2, starting transfers between devices, pull(): lax.ppermute(value, DP, [((i + steps) % N_DP, i) for i in range(N_DP)])  33.9 us
    all_to_all x3, starting transfers between devices, spread(): return lax.all_to_all(copies, axes, 0, 0, tiled=True)  21.2 us
    ppermute x2, starting transfers between devices, swap_cores(): return lax.ppermute(value, 'c', [(0, 1), (1, 0)])  11.1 us
    all_to_all x1, waiting for transfers between devices, shards(): lines = lax.all_to_all(lines, group, 0, 0, tiled=True)  10.6 us
    all_to_all x3, waiting for transfers between devices, spread(): return lax.all_to_all(copies, axes, 0, 0, tiled=True)  9.63 us
    dot_general x1, matrix products, branch(): jnp.dot(rows, projection, preferred_element_type=jnp.float32) + bias  6.51 us
    ppermute x2, starting transfers between devices, shards(): pieces.append(lax.ppermute(piece.astype(jnp.bfloat16), 'zl', ring))  6.18 us
  transfers between devices with their start and end apart: 10, of which 5 were waited for; matrix products, arithmetic and copies ran while one was open for 4% of the time, Pallas kernels for 0%

profile of v4, /device:TPU:1, one launch (start us, length us, event | category | flops | bytes accessed | tf_op | source)
XLA Modules:
  0.0 174.5 jit_solution(14357673752733192129)
XLA Ops:
  0.6 0.0 copy-start
  0.6 0.0 copy-start.7
  0.7 1.8 %broadcast_in_dim.31 = bf16[3,24,4096]{2,1,0:T(8,128)(2,1)} broadcast(bf16[24,4096]{1,0:T(8,128)(2,1)} %param.43), dimensions={1,2} | broadcast | bytes 786432 | tf_op jit(solution)/shard_map/broadcast_in_dim | solution.py:29
  2.5 6.0 %all-to-all-start = ((bf16[3,24,4096]{2,1,0:T(8,128)(2,1)}), bf16[3,24,4096]{2,1,0:T(8,128)(2,1)S(1)}, u32[]{:S(2)}, u32[]{:S(2)}) async-start(bf16[3,24,4096]{2,1,0:T(8,128)(2,1)} %broadcast_in_dim.31), calls=%async_computation | async-start | bytes 1179648 | tf_op jit(solution)/shard_map/all_to_all | solution.py:30
  9.2 0.0 copy-done
  9.2 0.2 dynamic-slice_reduce_fusion
  9.4 0.2 convert_reduce_fusion.4
  9.6 0.1 div.77
  9.7 0.1 select_n.154
  9.8 0.1 select_n.156
  9.9 0.1 pad.26.clone
  10.0 0.1 pad.23.clone
  10.1 0.0 copy-done.7
  10.1 27.4 %conditional.2 = (bf16[144,1408]{1,0:T(8,128)(2,1)S(1)}) conditional(s32[]{:T(128)} %clamp.7, bf16[144,1408]{1,0:T(8,128)(2,1)S(1)} %copy-done.7, bf16[144,1408]{1,0:T(8,128)(2,1)S(1)} %copy-done.7, bf16[144,1408]{1,0:T(8,128)(2,1)S(1)} %copy-done.7, bf16[144,1408]{1,0:T(8,128)(2,1)S(1)} %copy-done.7, ...), branch_computations={%region_1.2_spmd, %region_2.3_spmd, %region_3.4_spmd, %region_4.5_... | conditional | bytes 2433072 | solution.py:60
  10.1 6.7 %collective-permute-start.26 = (bf16[144,1408]{1,0:T(8,128)(2,1)S(1)}, bf16[144,1408]{1,0:T(8,128)(2,1)S(1)}, u32[]{:S(2)}, u32[]{:S(2)}) collective-permute-start(bf16[144,1408]{1,0:T(8,128)(2,1)S(1)} %param.27), channel_id=1, source_target_pairs={{648,0},{654,6},{660,12},{666,18},{672,24},{678,30},{684,36},{690,... | collective-permute-start | bytes 1216520 | tf_op jit(solution)/shard_map/cond/branch_27_fun/ppermute | solution.py:21
  16.8 20.7 %collective-permute-done.26 = bf16[144,1408]{1,0:T(8,128)(2,1)S(1)} collective-permute-done((bf16[144,1408]{1,0:T(8,128)(2,1)S(1)}, bf16[144,1408]{1,0:T(8,128)(2,1)S(1)}, u32[]{:S(2)}, u32[]{:S(2)}) %collective-permute-start.26) | collective-permute-done | bytes 405536 | tf_op jit(solution)/shard_map/cond/branch_27_fun/ppermute | solution.py:21
  37.5 0.1 pad_maximum_fusion.12
  37.6 0.0 all-to-all-done
  37.6 0.0 copy-done.8
  37.6 0.0 copy-done.13
  37.6 77.4 %conditional.3 = (f32[144,4096]{1,0:T(8,128)S(1)}, f32[]{:T(128)}, f32[1408]{0:T(1024)S(1)}, bf16[72,4096]{1,0:T(8,128)(2,1)}, f32[144,1]{0,1:T(1,128)}) conditional(s32[]{:T(128)} %clamp.6, (f32[144,1]{0,1:T(1,128)S(1)}, bf16[3,24,4096]{2,1,0:T(8,128)(2,1)S(1)}, f32[4096]{0:T(1024)S(1)}, ...), branch_computations={%region_34.0_spmd, %region_38.42_spmd, %region_42.46_spmd, %region... | conditional | flops 3332192256 | bytes 72424784 | solution.py:87
  37.9 27.3 %collective-permute-start.35 = (bf16[144,1408]{1,0:T(8,128)(2,1)S(1)}, bf16[144,1408]{1,0:T(8,128)(2,1)S(1)}, u32[]{:S(2)}, u32[]{:S(2)}) collective-permute-start(bf16[144,1408]{1,0:T(8,128)(2,1)S(1)} %get-tuple-element.141), channel_id=1, source_target_pairs={{12,0},{18,6},{24,12},{30,18},{36,24},{42,30},{48,36},{54,42},{60,... | collective-permute-start | bytes 1216520 | tf_op jit(solution)/shard_map/cond/branch_2_fun/ppermute | solution.py:21
  65.2 8.2 %collective-permute-start.34 = (bf16[72,4096]{1,0:T(8,128)(2,1)S(1)}, bf16[72,4096]{1,0:T(8,128)(2,1)S(1)}, u32[]{:S(2)}, u32[]{:S(2)}) collective-permute-start(bf16[72,4096]{1,0:T(8,128)(2,1)S(1)} %bitcast.132), channel_id=1, source_target_pairs={{0,1},{1,0},{2,3},{3,2},{4,5},{5,4},{6,7},{7,6},{8,9},{9,8},{10,11... | collective-permute-start | bytes 1769480 | tf_op jit(solution)/shard_map/cond/branch_2_fun/ppermute | solution.py:25
  73.4 29.0 %collective-permute-done.35 = bf16[144,1408]{1,0:T(8,128)(2,1)S(1)} collective-permute-done((bf16[144,1408]{1,0:T(8,128)(2,1)S(1)}, bf16[144,1408]{1,0:T(8,128)(2,1)S(1)}, u32[]{:S(2)}, u32[]{:S(2)}) %collective-permute-start.35) | collective-permute-done | bytes 405536 | tf_op jit(solution)/shard_map/cond/branch_2_fun/ppermute | solution.py:21
  102.5 0.0 collective-permute-done.34
  102.5 0.0 copy-start.3
  102.5 0.3 fusion.16
  102.8 0.0 slice-start.6
  102.9 0.0 slice-start.7
  102.9 0.0 slice-start.8
  102.9 6.5 %convolution_add_fusion.2 = f32[144,1408]{1,0:T(8,128)S(1)} fusion(bf16[4096,1408]{1,0:T(8,128)(2,1)} %get-tuple-element.138, f32[4096]{0:T(1024)S(1)} %get-tuple-element.137, f32[144]{0:T(256)S(1)} %add_rsqrt_fusion.2, bf16[72,4096]{1,0:T(8,128)(2,1)S(1)} %collective-permute-done.34, bf16[72,4096]{1,0:T(8,128)(2,1)S(1)} %bitcast.134, ...), kind=kOutput, calls=%fused_computation.46 | convolution fusion | flops 1665275904 | bytes 13547584 | tf_op jit(solution)/shard_map/cond/branch_2_fun/dot_general | solution.py:74
  109.4 1.0 convert_reduce_fusion.2
  110.4 0.0 slice-done.6
  110.4 0.1 slice-done.8
  110.5 3.8 %fusion.48 = f32[144,4096]{1,0:T(8,128)S(1)} fusion(bf16[144,1408]{1,0:T(8,128)(2,1)S(1)} %get-tuple-element.170, bf16[4096,1408]{1,0:T(8,128)(2,1)S(1)} %bitcast.122), kind=kOutput, calls=%fused_computation.131 | convolution fusion | flops 1660944384 | bytes 14299136 | tf_op jit(solution)/shard_map/cond/branch_2_fun/dot_general | solution.py:80
  115.0 0.9 slice.126
  115.9 1.5 multiply_reduce_fusion
  117.5 0.1 pad.25.clone
  117.6 2.9 %collective-permute-start.38 = (bf16[72,4096]{1,0:T(8,128)(2,1)}, bf16[72,4096]{1,0:T(8,128)(2,1)S(1)}, u32[]{:S(2)}, u32[]{:S(2)}) collective-permute-start(bf16[72,4096]{1,0:T(8,128)(2,1)} %slice.126), channel_id=1, source_target_pairs={{0,1},{1,0},{2,3},{3,2},{4,5},{5,4},{6,7},{7,6},{8,9},{9,8},{10,11... | collective-permute-start | bytes 1769480 | tf_op jit(solution)/shard_map/ppermute | solution.py:25
  120.4 0.1 maximum_maximum_fusion.1
  120.5 0.7 maximum_maximum_fusion
  121.2 3.7 %all-to-all-start.1 = ((f32[24,8,128]{2,1,0:T(8,128)}), f32[24,8,128]{2,1,0:T(8,128)S(1)}, u32[]{:S(2)}, u32[]{:S(2)}) async-start(f32[24,8,128]{2,1,0:T(8,128)} %maximum_maximum_fusion), calls=%async_computation.1 | async-start | bytes 196608 | tf_op jit(solution)/shard_map/all_to_all | solution.py:131
  125.0 0.0 copy-done.6
  125.0 0.2 fusion.38
  125.2 10.6 %all-to-all-done.1 = f32[24,8,128]{2,1,0:T(8,128)S(1)} async-done(((f32[24,8,128]{2,1,0:T(8,128)}), f32[24,8,128]{2,1,0:T(8,128)S(1)}, u32[]{:S(2)}, u32[]{:S(2)}) %all-to-all-start.1) | async-done | bytes 98336 | tf_op jit(solution)/shard_map/all_to_all | solution.py:131
  135.8 0.1 select_reduce_fusion
  136.0 0.7 broadcast_in_dim.39
  136.6 9.5 %all-to-all-start.2 = ((f32[32,8,128]{2,1,0:T(8,128)}), f32[32,8,128]{2,1,0:T(8,128)S(1)}, u32[]{:S(2)}, u32[]{:S(2)}) async-start(f32[32,8,128]{2,1,0:T(8,128)} %broadcast_in_dim.39), calls=%async_computation.2 | async-start | bytes 262144 | tf_op jit(solution)/shard_map/all_to_all | solution.py:30
  146.1 0.0 collective-permute-done.38
  146.2 0.1 convert_add_fusion
  146.3 1.0 copy-done.5
  147.3 2.4 %collective-permute-start.39 = (bf16[24,4096]{1,0:T(8,128)(2,1)S(1)}, bf16[24,4096]{1,0:T(8,128)(2,1)S(1)}, u32[]{:S(2)}, u32[]{:S(2)}) collective-permute-start(bf16[24,4096]{1,0:T(8,128)(2,1)S(1)} %get-tuple-element.185), channel_id=1, source_target_pairs={{0,2},{2,4},{4,0},{1,3},{3,5},{5,1},{6,8},{8,10},{10,6},{7,9},{9,1... | collective-permute-start | bytes 589832 | tf_op jit(solution)/shard_map/ppermute | solution.py:103
  149.7 3.8 %collective-permute-start.40 = (bf16[24,4096]{1,0:T(8,128)(2,1)S(1)}, bf16[24,4096]{1,0:T(8,128)(2,1)S(1)}, u32[]{:S(2)}, u32[]{:S(2)}) collective-permute-start(bf16[24,4096]{1,0:T(8,128)(2,1)S(1)} %get-tuple-element.186), channel_id=1, source_target_pairs={{0,4},{2,0},{4,2},{1,5},{3,1},{5,3},{6,10},{8,6},{10,8},{7,11},{9,... | collective-permute-start | bytes 589832 | tf_op jit(solution)/shard_map/ppermute | solution.py:103
  153.6 1.7 all-to-all-done.2
  155.3 0.6 broadcast_in_dim.40
  156.0 5.7 %all-to-all-start.3 = ((f32[24,8,128]{2,1,0:T(8,128)}), f32[24,8,128]{2,1,0:T(8,128)S(1)}, u32[]{:S(2)}, u32[]{:S(2)}) async-start(f32[24,8,128]{2,1,0:T(8,128)} %broadcast_in_dim.40), calls=%async_computation.3 | async-start | bytes 196608 | tf_op jit(solution)/shard_map/all_to_all | solution.py:30
  161.7 0.0 collective-permute-done.39
  161.7 0.0 collective-permute-done.40
  161.7 1.3 fusion.34
  163.0 1.8 %fusion.37 = bf16[24,4096]{1,0:T(8,128)(2,1)} fusion(bf16[24,4096]{1,0:T(8,128)(2,1)S(1)} %copy-done.6, f32[24]{0:T(128)S(1)} %broadcast_multiply_fusion.4, f32[24]{0:T(128)S(1)} %add_rsqrt_fusion.4, f32[4096]{0:T(1024)S(1)} %copy-done.8, bf16[24,4096]{1,0:T(8,128)(2,1)S(1)} %collective-permute-done.40, bf16[24,4096]{1,0:T(8,128)(2,1)S(1)} %collective-permute-done.39, ...), kind=kLoop, calls=%fused_computation.98 | loop fusion | flops 1081344 | bytes 1196228 | tf_op jit(solution)/shard_map/convert_element_type | solution.py:150
  164.8 7.9 %all-to-all-done.3 = f32[24,8,128]{2,1,0:T(8,128)S(1)} async-done(((f32[24,8,128]{2,1,0:T(8,128)}), f32[24,8,128]{2,1,0:T(8,128)S(1)}, u32[]{:S(2)}, u32[]{:S(2)}) %all-to-all-start.3) | async-done | bytes 98336 | tf_op jit(solution)/shard_map/all_to_all | solution.py:30
  172.7 0.6 slice_bitcast_fusion.8
  173.3 0.5 slice.78
  173.9 0.6 slice.74
  (32 shorter events, 0.3 us)
Async XLA Ops:
  0.6 8.6 %copy-start = (s32[128,144]{0,1:T(8,128)S(1)}, s32[128,144]{0,1:T(8,128)}, u32[]{:S(2)}) copy-start(s32[128,144]{0,1:T(8,128)} %param.44) | copy-start | bytes 221188
  0.6 9.4 %copy-start.7 = (bf16[144,1408]{1,0:T(8,128)(2,1)S(1)}, bf16[144,1408]{1,0:T(8,128)(2,1)}, u32[]{:S(2)}) copy-start(bf16[144,1408]{1,0:T(8,128)(2,1)} %param.45) | copy-start | bytes 1216516
  2.5 35.1 %all-to-all-start = ((bf16[3,24,4096]{2,1,0:T(8,128)(2,1)}), bf16[3,24,4096]{2,1,0:T(8,128)(2,1)S(1)}, u32[]{:S(2)}, u32[]{:S(2)}) async-start(bf16[3,24,4096]{2,1,0:T(8,128)(2,1)} %broadcast_in_dim.31), calls=%async_computation | async-start | bytes 1179648 | tf_op jit(solution)/shard_map/all_to_all | solution.py:30
  10.1 27.5 %copy-start.8 = (f32[4096]{0:T(1024)S(1)}, f32[4096]{0:T(1024)}, u32[]{:S(2)}) copy-start(f32[4096]{0:T(1024)} %param.47) | copy-start | bytes 49156
  10.1 27.5 %copy-start.13 = (f32[1408]{0:T(1024)S(1)}, f32[1408]{0:T(1024)}, u32[]{:S(2)}) copy-start(f32[1408]{0:T(1024)} %param.48) | copy-start | bytes 16900
  10.1 27.4 %collective-permute-start.26 = (bf16[144,1408]{1,0:T(8,128)(2,1)S(1)}, bf16[144,1408]{1,0:T(8,128)(2,1)S(1)}, u32[]{:S(2)}, u32[]{:S(2)}) collective-permute-start(bf16[144,1408]{1,0:T(8,128)(2,1)S(1)} %param.27), channel_id=1, source_target_pairs={{648,0},{654,6},{660,12},{666,18},{672,24},{678,30},{684,36},{690,... | collective-permute-start | bytes 1216520 | tf_op jit(solution)/shard_map/cond/branch_27_fun/ppermute | solution.py:21
  37.9 64.6 %collective-permute-start.35 = (bf16[144,1408]{1,0:T(8,128)(2,1)S(1)}, bf16[144,1408]{1,0:T(8,128)(2,1)S(1)}, u32[]{:S(2)}, u32[]{:S(2)}) collective-permute-start(bf16[144,1408]{1,0:T(8,128)(2,1)S(1)} %get-tuple-element.141), channel_id=1, source_target_pairs={{12,0},{18,6},{24,12},{30,18},{36,24},{42,30},{48,36},{54,42},{60,... | collective-permute-start | bytes 1216520 | tf_op jit(solution)/shard_map/cond/branch_2_fun/ppermute | solution.py:21
  65.2 37.3 %collective-permute-start.34 = (bf16[72,4096]{1,0:T(8,128)(2,1)S(1)}, bf16[72,4096]{1,0:T(8,128)(2,1)S(1)}, u32[]{:S(2)}, u32[]{:S(2)}) collective-permute-start(bf16[72,4096]{1,0:T(8,128)(2,1)S(1)} %bitcast.132), channel_id=1, source_target_pairs={{0,1},{1,0},{2,3},{3,2},{4,5},{5,4},{6,7},{7,6},{8,9},{9,8},{10,11... | collective-permute-start | bytes 1769480 | tf_op jit(solution)/shard_map/cond/branch_2_fun/ppermute | solution.py:25
  102.5 6.9 %copy-start.3 = (bf16[72,4096]{1,0:T(8,128)(2,1)}, bf16[72,4096]{1,0:T(8,128)(2,1)S(1)}, u32[]{:S(2)}) copy-start(bf16[72,4096]{1,0:T(8,128)(2,1)S(1)} %collective-permute-done.34) | copy-start | bytes 1769476 | tf_op jit(solution)/shard_map/cond
  102.8 6.6 %copy-start.11 = (f32[144]{0:T(256)}, f32[144]{0:T(256)S(1)}, u32[]{:S(2)}) copy-start(f32[144]{0:T(256)S(1)} %add_rsqrt_fusion.2) | copy-start | bytes 1732 | tf_op jit(solution)/shard_map/cond
  102.8 7.6 %slice-start.6 = ((s8[11534336]{0:T(1024)(128)(4,1)}), s8[4194304]{0:T(1024)(128)(4,1)S(1)}, s32[]{:S(2)}) async-start(s8[11534336]{0:T(1024)(128)(4,1)} %bitcast.121), calls=%async_computation.10 | async-start | bytes 8388608 | tf_op jit(solution)/shard_map/cond
  102.9 7.5 %slice-start.7 = ((s8[11534336]{0:T(1024)(128)(4,1)}), s8[4194304]{0:T(1024)(128)(4,1)S(1)}, s32[]{:S(2)}) async-start(s8[11534336]{0:T(1024)(128)(4,1)} %bitcast.121), calls=%async_computation.11 | async-start | bytes 8388608 | tf_op jit(solution)/shard_map/cond
  102.9 7.6 %slice-start.8 = ((s8[11534336]{0:T(1024)(128)(4,1)}), s8[3145728]{0:T(1024)(128)(4,1)S(1)}, s32[]{:S(2)}) async-start(s8[11534336]{0:T(1024)(128)(4,1)} %bitcast.121), calls=%async_computation.12 | async-start | bytes 6291456 | tf_op jit(solution)/shard_map/cond
  115.9 9.1 %copy-start.6 = (bf16[24,4096]{1,0:T(8,128)(2,1)S(1)}, bf16[24,4096]{1,0:T(8,128)(2,1)}, u32[]{:S(2)}) copy-start(bf16[24,4096]{1,0:T(8,128)(2,1)} %param.43) | copy-start | bytes 589828
  117.6 28.6 %collective-permute-start.38 = (bf16[72,4096]{1,0:T(8,128)(2,1)}, bf16[72,4096]{1,0:T(8,128)(2,1)S(1)}, u32[]{:S(2)}, u32[]{:S(2)}) collective-permute-start(bf16[72,4096]{1,0:T(8,128)(2,1)} %slice.126), channel_id=1, source_target_pairs={{0,1},{1,0},{2,3},{3,2},{4,5},{5,4},{6,7},{7,6},{8,9},{9,8},{10,11... | collective-permute-start | bytes 1769480 | tf_op jit(solution)/shard_map/ppermute | solution.py:25
  121.2 14.6 %all-to-all-start.1 = ((f32[24,8,128]{2,1,0:T(8,128)}), f32[24,8,128]{2,1,0:T(8,128)S(1)}, u32[]{:S(2)}, u32[]{:S(2)}) async-start(f32[24,8,128]{2,1,0:T(8,128)} %maximum_maximum_fusion), calls=%async_computation.1 | async-start | bytes 196608 | tf_op jit(solution)/shard_map/all_to_all | solution.py:131
  136.6 18.7 %all-to-all-start.2 = ((f32[32,8,128]{2,1,0:T(8,128)}), f32[32,8,128]{2,1,0:T(8,128)S(1)}, u32[]{:S(2)}, u32[]{:S(2)}) async-start(f32[32,8,128]{2,1,0:T(8,128)} %broadcast_in_dim.39), calls=%async_computation.2 | async-start | bytes 262144 | tf_op jit(solution)/shard_map/all_to_all | solution.py:30
  146.3 1.0 copy-start.5
  147.3 14.3 %collective-permute-start.39 = (bf16[24,4096]{1,0:T(8,128)(2,1)S(1)}, bf16[24,4096]{1,0:T(8,128)(2,1)S(1)}, u32[]{:S(2)}, u32[]{:S(2)}) collective-permute-start(bf16[24,4096]{1,0:T(8,128)(2,1)S(1)} %get-tuple-element.185), channel_id=1, source_target_pairs={{0,2},{2,4},{4,0},{1,3},{3,5},{5,1},{6,8},{8,10},{10,6},{7,9},{9,1... | collective-permute-start | bytes 589832 | tf_op jit(solution)/shard_map/ppermute | solution.py:103
  149.7 12.0 %collective-permute-start.40 = (bf16[24,4096]{1,0:T(8,128)(2,1)S(1)}, bf16[24,4096]{1,0:T(8,128)(2,1)S(1)}, u32[]{:S(2)}, u32[]{:S(2)}) collective-permute-start(bf16[24,4096]{1,0:T(8,128)(2,1)S(1)} %get-tuple-element.186), channel_id=1, source_target_pairs={{0,4},{2,0},{4,2},{1,5},{3,1},{5,3},{6,10},{8,6},{10,8},{7,11},{9,... | collective-permute-start | bytes 589832 | tf_op jit(solution)/shard_map/ppermute | solution.py:103
  156.0 16.7 %all-to-all-start.3 = ((f32[24,8,128]{2,1,0:T(8,128)}), f32[24,8,128]{2,1,0:T(8,128)S(1)}, u32[]{:S(2)}, u32[]{:S(2)}) async-start(f32[24,8,128]{2,1,0:T(8,128)} %broadcast_in_dim.40), calls=%async_computation.3 | async-start | bytes 196608 | tf_op jit(solution)/shard_map/all_to_all | solution.py:30
